TPU v7x, 32 devices: a whole 2x2x4 slice. The times are simulated.
32 devices in a mesh: tm: 4 (over z), width: 4 (over x, core), head: 2 (over y).
Axes of the slice: x: 2, y: 2, z: 4, core: 2. Of those that a mesh axis runs over, the one named last changes fastest.
Arguments:
- query_heads: bfloat16 [12, 36, 40, 256], P('tm', None, 'width', 'head'), may hold values from -18 to 18
- key_heads: bfloat16 [12, 36, 40, 256], P('tm', None, 'width', 'head'), may hold values from -18 to 18
- value_heads: bfloat16 [12, 36, 40, 256], P('tm', None, 'width', 'head'), may hold values from -10 to 10
- row_valid: int32 [36], replicated, may hold values from 0 to 1, as said below
- out_weight: bfloat16 [256, 3072], P(None, 'head'), may hold values from -0.375 to 0.375
- grad_mixed: bfloat16 [12, 36, 40, 3072], P('tm', None, 'width', 'head'), may hold values from -6 to 6
Outputs:
- mixed: bfloat16 [12, 36, 40, 3072], P('tm', None, 'width', 'head')
- grad_query: bfloat16 [12, 36, 40, 256], P('tm', None, 'width', 'head')
- grad_key: bfloat16 [12, 36, 40, 256], P('tm', None, 'width', 'head')
- grad_value: bfloat16 [12, 36, 40, 256], P('tm', None, 'width', 'head')
- grad_weight: float32 [256, 3072], P(('tm', 'width'), 'head')
Inputs may be any that keep to these rules, and one draw needn't show every extreme that they name: row_valid is 1 on every row before the last 9 rows; among the last 9 rows at least one is 1 and at least one is 0.
All inputs are finite; a program needn't handle non-finite values.
Results may differ from a plain program's by a relative error of at most 0.015.
Values may be sent and summed in bfloat16 or wider, within the bound.
A program may use at most 256 MiB of HBM per device.

v0:
```python
import math

import jax
import jax.numpy as jnp
from jax import lax
from jax.sharding import PartitionSpec as P

TH = 9


NEG_FILL = -1e30


def extended(cells, sides, width):
    for axis, dim in sides:
        count = lax.axis_size(axis)
        ends = count - 1
        head = lax.slice_in_dim(cells, 0, width, axis=dim)
        tail = lax.slice_in_dim(cells, cells.shape[dim] - width, cells.shape[dim], axis=dim)
        cells = jnp.concatenate(
            [
                lax.ppermute(tail, axis, [(i, (i + 1) % count) for i in range(ends)]),
                cells,
                lax.ppermute(head, axis, [((i + 1) % count, i) for i in range(ends)]),
            ],
            axis=dim,
        )
    return cells


def product_nt(left, right):
    return lax.dot_general(
        left, right, (((1,), (1,)), ((), ())), preferred_element_type=jnp.float32
    )


def product_tn(left, right):
    return lax.dot_general(
        left, right, (((0,), (0,)), ((), ())), preferred_element_type=jnp.float32
    )


def band_layout(tile_count):
    band_tiles = min(4, tile_count)
    layout = []
    for band_index in range(tile_count // 2):
        key_tile = min(max(2 * band_index - 1, 0), tile_count - band_tiles)
        layout.append((2 * band_index, key_tile, band_tiles))
    return layout


def tile_number(frames, rows, columns, row_start, tile_rows):
    row_ids = lax.broadcasted_iota(jnp.int32, (frames, rows, columns), 1)
    return ((row_ids + row_start) // tile_rows).reshape(-1)


def band_parts(query_block, key_wide, value_wide, live_wide, tile_rows, scale, entry):
    query_tile, key_tile, band_tiles = entry
    frames, rows, columns, depth = query_block.shape
    query_low = query_tile * tile_rows
    key_low = key_tile * tile_rows
    key_rows = band_tiles * tile_rows
    query_band = query_block[:, query_low : query_low + 2 * tile_rows].reshape(-1, depth)
    key_band = key_wide.reshape(-1, depth)
    value_band = value_wide.reshape(-1, depth)
    live_band = live_wide.reshape(-1)
    query_tiles = tile_number(frames, 2 * tile_rows, columns, query_low, tile_rows)
    key_tiles = tile_number(key_wide.shape[0], key_rows, key_wide.shape[2], key_low, tile_rows)
    allowed = live_band[None, :] & (jnp.abs(query_tiles[:, None] - key_tiles[None, :]) <= 1)
    scores = product_nt(query_band, key_band) * scale
    scores = jnp.where(allowed, scores, NEG_FILL)
    return (query_band, key_band, value_band, scores)


def attend_forward(query_block, key_wide, value_wide, live_wide, tile_rows, scale):
    frames, rows, columns, depth = query_block.shape
    outputs = []
    logs = []
    for entry in band_layout(rows // tile_rows):
        query_band, key_band, value_band, scores = band_parts(
            query_block, key_wide, value_wide, live_wide, tile_rows, scale, entry
        )
        peak = jnp.max(scores, axis=1, keepdims=True)
        expos = jnp.exp(scores - peak)
        totals = jnp.sum(expos, axis=1, keepdims=True)
        attended = (
            jnp.dot(expos.astype(jnp.bfloat16), value_band, preferred_element_type=jnp.float32)
            / totals
        )
        outputs.append(attended.astype(jnp.bfloat16).reshape(frames, 2 * tile_rows, columns, depth))
        logs.append((peak + jnp.log(totals)).reshape(frames, 2 * tile_rows, columns))
    return (jnp.concatenate(outputs, axis=1), jnp.concatenate(logs, axis=1))


def attend_backward(
    query_block,
    key_wide,
    value_wide,
    live_wide,
    lse_block,
    grad_block,
    delta_block,
    tile_rows,
    scale,
):
    frames, rows, columns, depth = query_block.shape
    wide_frames = key_wide.shape[0]
    wide_columns = key_wide.shape[2]
    grad_pair = jnp.zeros((2, wide_frames, rows, wide_columns, depth), jnp.float32)
    grad_parts = []
    for entry in band_layout(rows // tile_rows):
        query_tile, key_tile, band_tiles = entry
        query_low = query_tile * tile_rows
        key_low = key_tile * tile_rows
        key_rows = band_tiles * tile_rows
        query_band, key_band, value_band, scores = band_parts(
            query_block, key_wide, value_wide, live_wide, tile_rows, scale, entry
        )
        lse_band = lse_block[:, query_low : query_low + 2 * tile_rows].reshape(-1)
        delta_band = delta_block[:, query_low : query_low + 2 * tile_rows].reshape(-1)
        grad_band = grad_block[:, query_low : query_low + 2 * tile_rows].reshape(-1, depth)
        probs = jnp.exp(scores - lse_band[:, None])
        dprob = product_nt(grad_band, value_band)
        dscore = (probs * (dprob - delta_band[:, None]) * scale).astype(jnp.bfloat16)
        grad_query_band = jnp.dot(dscore, key_band, preferred_element_type=jnp.float32)
        grad_key_band = product_tn(dscore, query_band)
        grad_value_band = product_tn(probs.astype(jnp.bfloat16), grad_band)
        grad_pair = grad_pair.at[0, :, key_low : key_low + key_rows].add(
            grad_key_band.reshape(wide_frames, key_rows, wide_columns, depth)
        )
        grad_pair = grad_pair.at[1, :, key_low : key_low + key_rows].add(
            grad_value_band.reshape(wide_frames, key_rows, wide_columns, depth)
        )
        grad_parts.append(grad_query_band.reshape(frames, 2 * tile_rows, columns, depth))
    return (jnp.concatenate(grad_parts, axis=1), grad_pair)


def attend_keys(
    key_block,
    value_block,
    query_wide,
    grad_wide,
    lse_wide,
    delta_wide,
    query_ok,
    key_live,
    tile_rows,
    scale,
):
    frames, rows, columns, depth = key_block.shape
    wide_frames = query_wide.shape[0]
    wide_columns = query_wide.shape[2]
    key_parts = []
    value_parts = []
    for entry in band_layout(rows // tile_rows):
        key_tile, query_tile, band_tiles = entry
        key_low = key_tile * tile_rows
        query_low = query_tile * tile_rows
        query_rows = band_tiles * tile_rows
        key_band = key_block[:, key_low : key_low + 2 * tile_rows].reshape(-1, depth)
        value_band = value_block[:, key_low : key_low + 2 * tile_rows].reshape(-1, depth)
        live_band = key_live[:, key_low : key_low + 2 * tile_rows].reshape(-1)
        query_band = query_wide.reshape(-1, depth)
        grad_band = grad_wide.reshape(-1, depth)
        lse_band = lse_wide.reshape(-1)
        delta_band = delta_wide.reshape(-1)
        ok_band = query_ok.reshape(-1)
        query_tiles = tile_number(wide_frames, query_rows, wide_columns, query_low, tile_rows)
        key_tiles = tile_number(frames, 2 * tile_rows, columns, key_low, tile_rows)
        allowed = (
            ok_band[:, None]
            & live_band[None, :]
            & (jnp.abs(query_tiles[:, None] - key_tiles[None, :]) <= 1)
        )
        scores = jnp.where(allowed, product_nt(query_band, key_band) * scale, NEG_FILL)
        probs = jnp.exp(scores - lse_band[:, None])
        dprob = product_nt(grad_band, value_band)
        dscore = (probs * (dprob - delta_band[:, None]) * scale).astype(jnp.bfloat16)
        key_parts.append(
            product_tn(dscore, query_band).reshape(frames, 2 * tile_rows, columns, depth)
        )
        value_parts.append(
            product_tn(probs.astype(jnp.bfloat16), grad_band).reshape(
                frames, 2 * tile_rows, columns, depth
            )
        )
    return jnp.stack([jnp.concatenate(key_parts, axis=1), jnp.concatenate(value_parts, axis=1)])


def neighbour_tiles(paired, frames, columns):
    framed = extended(paired, (("tm", 1),), frames)
    return extended(framed, (("width", 3),), columns)


def shards(query_heads, key_heads, value_heads, row_valid, out_weight, grad_mixed):
    frames, rows, columns, depth = query_heads.shape
    scale = 1.0 / math.sqrt(depth)
    frame_total = lax.axis_size("tm") * frames
    column_total = lax.axis_size("width") * columns
    frame_ids = (lax.axis_index("tm") - 1) * frames + jnp.arange(3 * frames, dtype=jnp.int32)
    column_ids = (lax.axis_index("width") - 1) * columns + jnp.arange(3 * columns, dtype=jnp.int32)
    frame_ok = (frame_ids >= 0) & (frame_ids < frame_total)
    column_ok = (column_ids >= 0) & (column_ids < column_total)
    live_rows = row_valid > 0
    live_wide = frame_ok[:, None, None] & live_rows[None, :, None] & column_ok[None, None, :]
    paired = jnp.stack([key_heads, value_heads])
    wide_pair = neighbour_tiles(paired, frames, columns)
    key_wide = wide_pair[0]
    value_wide = wide_pair[1]
    attended, lse_block = attend_forward(query_heads, key_wide, value_wide, live_wide, TH, scale)
    heads_all = lax.all_gather(attended.reshape(-1, depth), "head", axis=1, tiled=True)
    grad_flat = grad_mixed.reshape(-1, grad_mixed.shape[-1])
    mixed = (
        jnp.dot(heads_all, out_weight, preferred_element_type=jnp.float32)
        .astype(jnp.bfloat16)
        .reshape(frames, rows, columns, -1)
    )
    grad_heads = product_nt(grad_flat, out_weight)
    grad_attended = lax.psum_scatter(
        grad_heads.astype(jnp.bfloat16), "head", scatter_dimension=1, tiled=True
    ).reshape(frames, rows, columns, depth)
    grad_weight = lax.psum_scatter(
        product_tn(heads_all, grad_flat), ("tm", "width"), scatter_dimension=0, tiled=True
    )
    delta_block = jnp.sum(grad_attended.astype(jnp.float32) * attended.astype(jnp.float32), axis=-1)
    grad_query, grad_pair = attend_backward(
        query_heads,
        key_wide,
        value_wide,
        live_wide,
        lse_block,
        grad_attended,
        delta_block,
        TH,
        scale,
    )
    query_pair = neighbour_tiles(jnp.stack([query_heads, grad_attended]), frames, columns)
    stats = jnp.stack([lse_block, delta_block])
    stats_framed = extended(stats, (("tm", 1),), frames)
    stats_wide = extended(stats_framed, (("width", 3),), columns)
    query_ok = jnp.broadcast_to(
        frame_ok[:, None, None] & column_ok[None, None, :], (3 * frames, rows, 3 * columns)
    )
    key_live = jnp.broadcast_to(live_rows[None, :, None], (frames, rows, columns))
    owned = attend_keys(
        key_heads,
        value_heads,
        query_pair[0],
        query_pair[1],
        stats_wide[0],
        stats_wide[1],
        query_ok,
        key_live,
        TH,
        scale,
    )
    return (
        mixed,
        grad_query.astype(jnp.bfloat16),
        owned[0].astype(jnp.bfloat16),
        owned[1].astype(jnp.bfloat16),
        grad_weight,
    )


def solution(mesh):
    return jax.shard_map(
        shards,
        mesh=mesh,
        in_specs=(
            P("tm", None, "width", "head"),
            P("tm", None, "width", "head"),
            P("tm", None, "width", "head"),
            P(),
            P(None, "head"),
            P("tm", None, "width", "head"),
        ),
        out_specs=(
            P("tm", None, "width", "head"),
            P("tm", None, "width", "head"),
            P("tm", None, "width", "head"),
            P("tm", None, "width", "head"),
            P(("tm", "width"), "head"),
        ),
        check_vma=False,
    )
```

profile of v0, /device:TPU:0, one launch (start us, length us, event | category | flops | bytes accessed | tf_op | source)
XLA Modules:
  0.0 509.4 jit_solution(14358203647157526699)
XLA Ops:
  11.0 6.4 %collective-permute-start = (bf16[2,3,36,10,128]{4,0,3,2,1:T(2,128)(2,1)S(1)}, bf16[2,3,36,10,128]{4,0,3,2,1:T(2,128)(2,1)}, u32[]{:S(2)}, u32[]{:S(2)}) collective-permute-start(bf16[2,3,36,10,128]{4,0,3,2,1:T(2,128)(2,1)S(1)} %copy.67), channel_id=1, source_target_pairs={{0,8},{8,16},{16,24},{1,9},{9,17},{17,25},{2,10},{10,18},{18,26},{... | collective-permute-start | bytes 1658888 | tf_op jit(solution)/shard_map/ppermute | solution.py:22
  17.4 5.8 %copy.79 = bf16[3,36,10,1536]{3,2,1,0:T(8,128)(2,1)} copy(bf16[3,36,10,1536]{3,1,2,0:T(8,128)(2,1)} %param.11) | data formatting | bytes 6635520 | tf_op args[5]
  23.2 6.8 %reshape.366 = bf16[1080,1536]{1,0:T(8,128)(2,1)} reshape(bf16[3,36,10,1536]{3,2,1,0:T(8,128)(2,1)} %copy.79) | data formatting | bytes 6635520 | tf_op jit(solution)/shard_map/reshape | solution.py:212
  30.0 3.0 convolution_convert_fusion.1
  39.3 2.5 copy.71
  43.1 4.2 collective-permute-start.2
  56.3 5.6 %collective-permute-start.4 = (bf16[2,3,36,10,128]{4,0,3,2,1:T(2,128)(2,1)}, bf16[2,3,36,10,128]{4,0,3,2,1:T(2,128)(2,1)}, u32[]{:S(2)}, u32[]{:S(2)}) collective-permute-start(bf16[2,3,36,10,128]{4,0,3,2,1:T(2,128)(2,1)} %copy.81), channel_id=1, source_target_pairs={{0,8},{8,16},{16,24},{1,9},{9,17},{17,25},{2,10},{10,18},{18,26},{... | collective-permute-start | bytes 1658888 | tf_op jit(solution)/shard_map/ppermute | solution.py:22
  104.4 3.7 copy.85
  109.4 4.3 collective-permute-start.6
  117.1 3.6 pad_maximum_fusion
  120.7 2.5 fusion.65
  128.3 3.8 copy.77
  132.1 4.0 reshape_squeeze.9
  136.1 10.0 %fusion.74 = (f32[540]{0:T(1024)S(1)}, f32[540,9720]{1,0:T(8,128)S(1)}) fusion(bf16[9720,128]{1,0:T(8,128)(2,1)} %reshape_squeeze.8, bf16[540,128]{1,0:T(8,128)(2,1)} %reshape.362, s32[9720]{0:T(1024)S(1)} %copy-done.35, s32[540]{0:T(1024)S(1)} %copy-done.42, pred[9720]{0:T(1024)(128)(4,1)S(1)} %copy-done.38), kind=kOutput, calls=%fused_computation.108 | convolution fusion | flops 1380433792 | bytes 23674680 | tf_op jit(solution)/shard_map/dot_general | solution.py:32
  146.1 4.1 fusion.14
  150.2 3.0 copy-done.3
  153.8 10.8 %fusion.61 = bf16[540,128]{1,0:T(8,128)(2,1)} fusion(bf16[9720,128]{1,0:T(8,128)(2,1)S(1)} %reshape_squeeze.9, f32[540,9720]{1,0:T(8,128)} %copy-done.3, f32[540]{0:T(1024)S(1)} %get-tuple-element.43, f32[540]{0:T(1024)S(1)} %fusion.14), kind=kOutput, calls=%fused_computation.61 | convolution fusion | flops 1354328576 | bytes 23626080 | tf_op jit(solution)/shard_map/dot_general | solution.py:87
  164.6 8.4 %fusion.75 = (f32[540]{0:T(1024)S(1)}, f32[540,9720]{1,0:T(8,128)S(1)}) fusion(bf16[9720,128]{1,0:T(8,128)(2,1)S(1)} %copy-done.23, bf16[540,128]{1,0:T(8,128)(2,1)S(1)} %copy-done.33, s32[9720]{0:T(1024)S(1)} %copy-done.35, s32[540]{0:T(1024)S(1)} %copy-done.40, pred[9720]{0:T(1024)(128)(4,1)S(1)} %copy-done.38), kind=kOutput, calls=%fused_computation.109 | convolution fusion | flops 1380433792 | bytes 23674680 | tf_op jit(solution)/shard_map/dot_general | solution.py:32
  173.0 7.0 %copy-done.2 = f32[540,9720]{1,0:T(8,128)} copy-done((f32[540,9720]{1,0:T(8,128)}, f32[540,9720]{1,0:T(8,128)S(1)}, u32[]{:S(2)}) %copy-start.2) | copy-done | bytes 20995224
  180.1 3.9 fusion.12
  183.9 10.7 %fusion.55 = bf16[540,128]{1,0:T(8,128)(2,1)} fusion(bf16[9720,128]{1,0:T(8,128)(2,1)S(1)} %reshape_squeeze.9, f32[540,9720]{1,0:T(8,128)} %copy-done.2, f32[540]{0:T(1024)S(1)} %get-tuple-element.45, f32[540]{0:T(1024)S(1)} %fusion.12), kind=kOutput, calls=%fused_computation.59 | convolution fusion | flops 1354328576 | bytes 23626080 | tf_op jit(solution)/shard_map/dot_general | solution.py:87
  209.7 5.1 %collective-permute-start.8 = (f32[2,3,36,10]{2,0,3,1:T(2,128)}, f32[2,3,36,10]{2,0,3,1:T(2,128)}, u32[]{:S(2)}, u32[]{:S(2)}) collective-permute-start(f32[2,3,36,10]{2,0,3,1:T(2,128)} %pad_maximum_fusion.12), channel_id=1, source_target_pairs={{0,8},{8,16},{16,24},{1,9},{9,17},{17,25},{2,10},{10,18},{18,26},{... | collective-permute-start | bytes 25928 | tf_op jit(solution)/shard_map/ppermute | solution.py:22
  215.0 12.4 %multiply_convert_fusion = bf16[540,9720]{1,0:T(8,128)(2,1)} fusion(f32[540,9720]{1,0:T(8,128)} %copy-done.3, bf16[540,128]{1,0:T(8,128)(2,1)} %reshape.369, bf16[9720,128]{1,0:T(8,128)(2,1)S(1)} %reshape_squeeze.9, f32[540]{0:T(1024)S(1)} %sub.240, f32[540]{0:T(1024)} %log_add_fusion), kind=kOutput, calls=%fused_computation.16 | convolution fusion | flops 1369936640 | bytes 34123680 | tf_op jit(solution)/shard_map/dot_general | solution.py:32
  227.4 16.0 %dot_general.81 = bf16[3,18,10,9720]{3,2,1,0:T(8,128)(2,1)} reshape(bf16[540,9720]{1,0:T(8,128)(2,1)} %multiply_convert_fusion) | data formatting | bytes 20995200 | tf_op jit(solution)/shard_map/dot_general | solution.py:125
  243.5 12.2 %multiply_convert_fusion.1 = bf16[540,9720]{1,0:T(8,128)(2,1)} fusion(f32[540,9720]{1,0:T(8,128)} %copy-done.2, bf16[540,128]{1,0:T(8,128)(2,1)S(1)} %copy-done.25, bf16[9720,128]{1,0:T(8,128)(2,1)S(1)} %reshape_squeeze.9, f32[540]{0:T(1024)S(1)} %sub.235, f32[540]{0:T(1024)S(1)} %copy-done.30), kind=kOutput, calls=%fused_computation.17 | convolution fusion | flops 1369936640 | bytes 34123680 | tf_op jit(solution)/shard_map/dot_general | solution.py:32
  255.8 16.1 %dot_general.78 = bf16[3,18,10,9720]{3,2,1,0:T(8,128)(2,1)} reshape(bf16[540,9720]{1,0:T(8,128)(2,1)} %multiply_convert_fusion.1) | data formatting | bytes 20995200 | tf_op jit(solution)/shard_map/dot_general | solution.py:125
  271.9 9.0 %fusion.37 = bf16[3,18,10,128]{3,2,1,0:T(8,128)(2,1)} fusion(bf16[3,18,10,9720]{3,2,1,0:T(8,128)(2,1)} %dot_general.81, bf16[9720,128,1,1]{1,0,2,3:T(8,128)(2,1)S(1)} %copy-done.20), kind=kOutput, calls=%fused_computation.53 | convolution fusion | flops 1343761920 | bytes 13124160 | tf_op jit(solution)/shard_map/dot_general | solution.py:125
  282.5 5.2 %fusion.34 = bf16[3,18,10,128]{3,2,1,0:T(8,128)(2,1)} fusion(bf16[3,18,10,9720]{3,2,1,0:T(8,128)(2,1)S(1)} %copy-done.4, bf16[9720,128,1,1]{1,0,2,3:T(8,128)(2,1)S(1)} %copy-done.20), kind=kOutput, calls=%fused_computation.52 | convolution fusion | flops 1343761920 | bytes 13124160 | tf_op jit(solution)/shard_map/dot_general | solution.py:125
  287.7 8.6 %all_gather.3 = bf16[1080,256]{1,0:T(8,128)(2,1)S(1)} all-gather(bf16[1080,128]{1,0:T(8,128)(2,1)S(1)} %copy-done.19), channel_id=1, replica_groups=mesh['tm'=4,'width'=4,'head'=2] {'head'}, dimensions={1}, use_global_device_ids=true | all-gather | bytes 829440 | tf_op jit(solution)/shard_map/all_gather | solution.py:211
  298.8 2.7 convolution_convert_fusion
  303.6 3.8 collective-permute-start.10
  307.6 6.6 %reshape.365 = bf16[3,36,10,1536]{3,2,1,0:T(8,128)(2,1)} reshape(bf16[1080,1536]{1,0:T(8,128)(2,1)} %convolution_convert_fusion) | data formatting | bytes 6635520 | tf_op jit(solution)/shard_map/reshape | solution.py:216
  314.1 6.3 %copy.99 = bf16[3,36,10,1536]{3,1,2,0:T(8,128)(2,1)} copy(bf16[3,36,10,1536]{3,2,1,0:T(8,128)(2,1)} %reshape.365) | data formatting | bytes 6635520
  328.0 3.3 pad_maximum_fusion.1
  338.3 3.6 reshape_squeeze.11
  341.9 4.9 reshape.376
  346.8 17.3 %fusion.76 = (bf16[540,9720]{1,0:T(8,128)(2,1)}, f32[540,9720]{1,0:T(8,128)}) fusion(f32[9720]{0:T(1024)S(1)} %sub.244, bf16[9720,128]{1,0:T(8,128)(2,1)} %reshape_squeeze.10, bf16[540,128]{1,0:T(8,128)(2,1)S(1)} %copy-done.31, s32[540]{0:T(1024)S(1)} %copy-done.43, s32[9720]{0:T(1024)S(1)} %copy-done.36, pred[540]{0:T(1024)(128)(4,1)S(1)} %copy-done.44, ...), kind=kOutput, calls=%fused_computation.110 | convolution fusion | flops 1390931840 | bytes 34209540 | tf_op jit(solution)/shard_map/dot_general | solution.py:32
  364.1 12.2 %fusion.1 = bf16[540,9720]{1,0:T(8,128)(2,1)} fusion(f32[540,9720]{1,0:T(8,128)} %get-tuple-element.48, bf16[9720,128]{1,0:T(8,128)(2,1)S(1)} %reshape_squeeze.11, bf16[540,128]{1,0:T(8,128)(2,1)S(1)} %copy-done.26, f32[9720]{0:T(1024)S(1)} %sub.247), kind=kOutput, calls=%fused_computation.2 | convolution fusion | flops 1364687872 | bytes 34158240 | tf_op jit(solution)/shard_map/dot_general | solution.py:32
  376.3 16.1 %dot_general.89 = bf16[3,18,10,9720]{3,2,1,0:T(8,128)(2,1)} reshape(bf16[540,9720]{1,0:T(8,128)(2,1)} %fusion.1) | data formatting | bytes 20995200 | tf_op jit(solution)/shard_map/dot_general | solution.py:38
  392.4 17.1 %fusion.77 = (bf16[540,9720]{1,0:T(8,128)(2,1)}, f32[540,9720]{1,0:T(8,128)}) fusion(f32[9720]{0:T(1024)S(1)} %sub.244, bf16[9720,128]{1,0:T(8,128)(2,1)} %reshape_squeeze.10, bf16[540,128]{1,0:T(8,128)(2,1)S(1)} %copy-done.32, s32[540]{0:T(1024)S(1)} %copy-done.41, s32[9720]{0:T(1024)S(1)} %copy-done.36, pred[540]{0:T(1024)(128)(4,1)S(1)} %copy-done.45, ...), kind=kOutput, calls=%fused_computation.111 | convolution fusion | flops 1390931840 | bytes 34209540 | tf_op jit(solution)/shard_map/dot_general | solution.py:32
  409.5 12.0 %fusion.5 = bf16[540,9720]{1,0:T(8,128)(2,1)} fusion(f32[540,9720]{1,0:T(8,128)} %get-tuple-element.50, bf16[9720,128]{1,0:T(8,128)(2,1)S(1)} %reshape_squeeze.11, bf16[540,128]{1,0:T(8,128)(2,1)S(1)} %copy-done.27, f32[9720]{0:T(1024)S(1)} %sub.247), kind=kOutput, calls=%fused_computation.8 | convolution fusion | flops 1364687872 | bytes 34158240 | tf_op jit(solution)/shard_map/dot_general | solution.py:32
  421.4 16.1 %dot_general.85 = bf16[3,18,10,9720]{3,2,1,0:T(8,128)(2,1)} reshape(bf16[540,9720]{1,0:T(8,128)(2,1)} %fusion.5) | data formatting | bytes 20995200 | tf_op jit(solution)/shard_map/dot_general | solution.py:38
  437.6 8.5 %fusion.43 = bf16[3,18,10,128]{3,2,1,0:T(8,128)(2,1)S(1)} fusion(bf16[3,18,10,9720]{3,2,1,0:T(8,128)(2,1)} %dot_general.89, bf16[9720,128,1,1]{1,0,2,3:T(8,128)(2,1)S(1)} %copy-done.22), kind=kOutput, calls=%fused_computation.55 | convolution fusion | flops 1343761920 | bytes 13124160 | tf_op jit(solution)/shard_map/dot_general | solution.py:38
  448.1 4.5 fusion.40
  453.5 16.0 %dot_general.93 = bf16[3,18,10,9720]{3,2,1,0:T(8,128)(2,1)} reshape(bf16[540,9720]{1,0:T(8,128)(2,1)} %get-tuple-element.47) | data formatting | bytes 20995200 | tf_op jit(solution)/shard_map/dot_general | solution.py:38
  469.5 16.1 %dot_general.91 = bf16[3,18,10,9720]{3,2,1,0:T(8,128)(2,1)} reshape(bf16[540,9720]{1,0:T(8,128)(2,1)} %get-tuple-element.49) | data formatting | bytes 20995200 | tf_op jit(solution)/shard_map/dot_general | solution.py:38
  485.6 8.3 %fusion.49 = bf16[3,18,10,128]{3,2,1,0:T(8,128)(2,1)S(1)} fusion(bf16[3,18,10,9720]{3,2,1,0:T(8,128)(2,1)} %dot_general.93, bf16[9720,128,1,1]{1,0,2,3:T(8,128)(2,1)S(1)} %copy-done.21), kind=kOutput, calls=%fused_computation.57 | convolution fusion | flops 1343761920 | bytes 13124160 | tf_op jit(solution)/shard_map/dot_general | solution.py:38
  496.2 4.5 fusion.46
  (219 shorter events, 114.1 us)
Async XLA Ops:
  8.0 22.0 %copy-start = (bf16[256,1536]{1,0:T(8,128)(2,1)S(1)}, bf16[256,1536]{1,0:T(8,128)(2,1)}, u32[]{:S(2)}) copy-start(bf16[256,1536]{1,0:T(8,128)(2,1)} %param.10) | copy-start | bytes 2359300
  8.0 42.3 %reduce-scatter.7.cloned.1.call-start = ((), (), s32[]{:S(2)}) async-start(), calls=%async_computation.3 | async-start | bytes 884736
  9.7 27.1 %collective-permute-start.1 = (bf16[2,3,36,10,128]{4,0,3,2,1:T(2,128)(2,1)S(1)}, bf16[2,3,36,10,128]{4,0,3,2,1:T(2,128)(2,1)}, u32[]{:S(2)}, u32[]{:S(2)}) collective-permute-start(bf16[2,3,36,10,128]{4,0,3,2,1:T(2,128)(2,1)S(1)} %copy.67), channel_id=1, source_target_pairs={{8,0},{16,8},{24,16},{9,1},{17,9},{25,17},{10,2},{18,10},{26,18},{... | collective-permute-start | bytes 1658888 | tf_op jit(solution)/shard_map/ppermute | solution.py:24
  11.0 26.9 %collective-permute-start = (bf16[2,3,36,10,128]{4,0,3,2,1:T(2,128)(2,1)S(1)}, bf16[2,3,36,10,128]{4,0,3,2,1:T(2,128)(2,1)}, u32[]{:S(2)}, u32[]{:S(2)}) collective-permute-start(bf16[2,3,36,10,128]{4,0,3,2,1:T(2,128)(2,1)S(1)} %copy.67), channel_id=1, source_target_pairs={{0,8},{8,16},{16,24},{1,9},{9,17},{17,25},{2,10},{10,18},{18,26},{... | collective-permute-start | bytes 1658888 | tf_op jit(solution)/shard_map/ppermute | solution.py:22
  23.2 11.1 %copy-start.46 = (s32[36]{0:T(128)S(1)}, s32[36]{0:T(128)}, u32[]{:S(2)}) copy-start(s32[36]{0:T(128)} %param.9) | copy-start | bytes 436
  23.2 15.9 %copy-start.15 = (bf16[3,36,10,128]{3,1,2,0:T(8,128)(2,1)S(1)}, bf16[3,36,10,128]{3,1,2,0:T(8,128)(2,1)}, u32[]{:S(2)}) copy-start(bf16[3,36,10,128]{3,1,2,0:T(8,128)(2,1)} %param.8) | copy-start | bytes 829444
  23.2 15.9 %copy-start.16 = (bf16[3,36,10,128]{3,1,2,0:T(8,128)(2,1)S(1)}, bf16[3,36,10,128]{3,1,2,0:T(8,128)(2,1)}, u32[]{:S(2)}) copy-start(bf16[3,36,10,128]{3,1,2,0:T(8,128)(2,1)} %param.7) | copy-start | bytes 829444
  30.0 17.4 %copy-start.24 = (bf16[3,36,10,128]{3,1,2,0:T(8,128)(2,1)S(1)}, bf16[3,36,10,128]{3,1,2,0:T(8,128)(2,1)}, u32[]{:S(2)}) copy-start(bf16[3,36,10,128]{3,1,2,0:T(8,128)(2,1)} %param.6) | copy-start | bytes 829444
  34.2 467.4 %reduce-scatter.5.cloned.1.call-start = ((), (), s32[]{:S(2)}) async-start(), calls=%async_computation.2 | async-start | bytes 1671168 | tf_op jit(solution)/shard_map/reduce_scatter | solution.py:222
  41.8 71.8 %collective-permute-start.3 = (bf16[2,9,36,10,128]{4,0,3,2,1:T(2,128)(2,1)}, bf16[2,9,36,10,128]{4,0,3,2,1:T(2,128)(2,1)}, u32[]{:S(2)}, u32[]{:S(2)}) collective-permute-start(bf16[2,9,36,10,128]{4,0,3,2,1:T(2,128)(2,1)} %copy.71), channel_id=1, source_target_pairs={{2,0},{4,2},{6,4},{3,1},{5,3},{7,5},{10,8},{12,10},{14,12},{11,9},... | collective-permute-start | bytes 4976648 | tf_op jit(solution)/shard_map/ppermute | solution.py:24
  43.1 72.2 %collective-permute-start.2 = (bf16[2,9,36,10,128]{4,0,3,2,1:T(2,128)(2,1)}, bf16[2,9,36,10,128]{4,0,3,2,1:T(2,128)(2,1)}, u32[]{:S(2)}, u32[]{:S(2)}) collective-permute-start(bf16[2,9,36,10,128]{4,0,3,2,1:T(2,128)(2,1)} %copy.71), channel_id=1, source_target_pairs={{0,2},{2,4},{4,6},{1,3},{3,5},{5,7},{8,10},{10,12},{12,14},{9,11},... | collective-permute-start | bytes 4976648 | tf_op jit(solution)/shard_map/ppermute | solution.py:22
  47.5 56.9 %copy-start.11 = (bf16[3,36,10,128]{3,2,1,0:T(8,128)(2,1)}, bf16[3,36,10,128]{3,2,1,0:T(8,128)(2,1)S(1)}, u32[]{:S(2)}) copy-start(bf16[3,36,10,128]{3,2,1,0:T(8,128)(2,1)S(1)} %copy.109) | copy-start | bytes 829444
  53.2 54.9 %copy-start.13 = (bf16[1,3,36,10,128]{4,3,2,1,0:T(8,128)(2,1)}, bf16[1,3,36,10,128]{4,3,2,1,0:T(8,128)(2,1)S(1)}, u32[]{:S(2)}) copy-start(bf16[1,3,36,10,128]{4,3,2,1,0:T(8,128)(2,1)S(1)} %stack_reshape.3) | copy-start | bytes 829444
  55.0 45.1 %collective-permute-start.5 = (bf16[2,3,36,10,128]{4,0,3,2,1:T(2,128)(2,1)}, bf16[2,3,36,10,128]{4,0,3,2,1:T(2,128)(2,1)}, u32[]{:S(2)}, u32[]{:S(2)}) collective-permute-start(bf16[2,3,36,10,128]{4,0,3,2,1:T(2,128)(2,1)} %copy.81), channel_id=1, source_target_pairs={{8,0},{16,8},{24,16},{9,1},{17,9},{25,17},{10,2},{18,10},{26,18},{... | collective-permute-start | bytes 1658888 | tf_op jit(solution)/shard_map/ppermute | solution.py:24
  56.3 45.0 %collective-permute-start.4 = (bf16[2,3,36,10,128]{4,0,3,2,1:T(2,128)(2,1)}, bf16[2,3,36,10,128]{4,0,3,2,1:T(2,128)(2,1)}, u32[]{:S(2)}, u32[]{:S(2)}) collective-permute-start(bf16[2,3,36,10,128]{4,0,3,2,1:T(2,128)(2,1)} %copy.81), channel_id=1, source_target_pairs={{0,8},{8,16},{16,24},{1,9},{9,17},{17,25},{2,10},{10,18},{18,26},{... | collective-permute-start | bytes 1658888 | tf_op jit(solution)/shard_map/ppermute | solution.py:22
  108.1 215.8 %collective-permute-start.7 = (bf16[2,9,36,10,128]{4,0,3,2,1:T(2,128)(2,1)}, bf16[2,9,36,10,128]{4,0,3,2,1:T(2,128)(2,1)}, u32[]{:S(2)}, u32[]{:S(2)}) collective-permute-start(bf16[2,9,36,10,128]{4,0,3,2,1:T(2,128)(2,1)} %copy.85), channel_id=1, source_target_pairs={{2,0},{4,2},{6,4},{3,1},{5,3},{7,5},{10,8},{12,10},{14,12},{11,9},... | collective-permute-start | bytes 4976648 | tf_op jit(solution)/shard_map/ppermute | solution.py:24
  109.4 216.5 %collective-permute-start.6 = (bf16[2,9,36,10,128]{4,0,3,2,1:T(2,128)(2,1)}, bf16[2,9,36,10,128]{4,0,3,2,1:T(2,128)(2,1)}, u32[]{:S(2)}, u32[]{:S(2)}) collective-permute-start(bf16[2,9,36,10,128]{4,0,3,2,1:T(2,128)(2,1)} %copy.85), channel_id=1, source_target_pairs={{0,2},{2,4},{4,6},{1,3},{3,5},{5,7},{8,10},{10,12},{12,14},{9,11},... | collective-permute-start | bytes 4976648 | tf_op jit(solution)/shard_map/ppermute | solution.py:22
  123.7 12.4 %copy-start.35 = (s32[9720]{0:T(1024)S(1)}, s32[9720]{0:T(1024)}, u32[]{:S(2)}) copy-start(s32[9720]{0:T(1024)} %select_n.98) | copy-start | bytes 116644
  123.7 12.4 %copy-start.38 = (pred[9720]{0:T(1024)(128)(4,1)S(1)}, pred[9720]{0:T(1024)(128)(4,1)}, u32[]{:S(2)}) copy-start(pred[9720]{0:T(1024)(128)(4,1)} %and.204) | copy-start | bytes 29164
  123.7 12.4 %copy-start.42 = (s32[540]{0:T(1024)S(1)}, s32[540]{0:T(1024)}, u32[]{:S(2)}) copy-start(s32[540]{0:T(1024)} %select_n.101) | copy-start | bytes 6484
  183.9 18.3 %copy-start.17 = (bf16[1080,128]{1,0:T(8,128)(2,1)S(1)}, bf16[1080,128]{1,0:T(8,128)(2,1)}, u32[]{:S(2)}) copy-start(bf16[1080,128]{1,0:T(8,128)(2,1)} %copy.107) | copy-start | bytes 829444
  208.4 93.1 %collective-permute-start.9 = (f32[2,3,36,10]{2,0,3,1:T(2,128)}, f32[2,3,36,10]{2,0,3,1:T(2,128)S(1)}, u32[]{:S(2)}, u32[]{:S(2)}) collective-permute-start(f32[2,3,36,10]{2,0,3,1:T(2,128)} %pad_maximum_fusion.12), channel_id=1, source_target_pairs={{8,0},{16,8},{24,16},{9,1},{17,9},{25,17},{10,2},{18,10},{26,18},{... | collective-permute-start | bytes 25928 | tf_op jit(solution)/shard_map/ppermute | solution.py:24
  209.7 91.8 %collective-permute-start.8 = (f32[2,3,36,10]{2,0,3,1:T(2,128)}, f32[2,3,36,10]{2,0,3,1:T(2,128)}, u32[]{:S(2)}, u32[]{:S(2)}) collective-permute-start(f32[2,3,36,10]{2,0,3,1:T(2,128)} %pad_maximum_fusion.12), channel_id=1, source_target_pairs={{0,8},{8,16},{16,24},{1,9},{9,17},{17,25},{2,10},{10,18},{18,26},{... | collective-permute-start | bytes 25928 | tf_op jit(solution)/shard_map/ppermute | solution.py:22
  227.3 16.2 %copy-start.25 = (bf16[540,128]{1,0:T(8,128)(2,1)S(1)}, bf16[540,128]{1,0:T(8,128)(2,1)}, u32[]{:S(2)}) copy-start(bf16[540,128]{1,0:T(8,128)(2,1)} %reshape.368) | copy-start | bytes 414724
  227.4 16.2 %copy-start.30 = (f32[540]{0:T(1024)S(1)}, f32[540]{0:T(1024)}, u32[]{:S(2)}) copy-start(f32[540]{0:T(1024)} %log_add_fusion.1) | copy-start | bytes 6484
  255.8 16.1 %copy-start.20 = (bf16[9720,128,1,1]{1,0,2,3:T(8,128)(2,1)S(1)}, bf16[9720,128,1,1]{1,0,2,3:T(8,128)(2,1)}, u32[]{:S(2)}) copy-start(bf16[9720,128,1,1]{1,0,2,3:T(8,128)(2,1)} %reshape.374) | copy-start | bytes 7464964
  282.5 13.8 %copy-start.18 = (bf16[1080,1536]{1,0:T(8,128)(2,1)S(1)}, bf16[1080,1536]{1,0:T(8,128)(2,1)}, u32[]{:S(2)}) copy-start(bf16[1080,1536]{1,0:T(8,128)(2,1)} %reshape.366) | copy-start | bytes 9953284
  287.7 19.7 %copy-start.28 = (bf16[3,18,10,128]{3,2,1,0:T(8,128)(2,1)S(1)}, bf16[3,18,10,128]{3,2,1,0:T(8,128)(2,1)}, u32[]{:S(2)}) copy-start(bf16[3,18,10,128]{3,2,1,0:T(8,128)(2,1)} %fusion.37) | copy-start | bytes 414724
  287.7 19.8 %copy-start.29 = (bf16[3,18,10,128]{3,2,1,0:T(8,128)(2,1)S(1)}, bf16[3,18,10,128]{3,2,1,0:T(8,128)(2,1)}, u32[]{:S(2)}) copy-start(bf16[3,18,10,128]{3,2,1,0:T(8,128)(2,1)} %fusion.34) | copy-start | bytes 414724
  302.3 19.0 %collective-permute-start.11 = (f32[2,9,36,10]{2,0,3,1:T(2,128)S(1)}, f32[2,9,36,10]{2,0,3,1:T(2,128)S(1)}, u32[]{:S(2)}, u32[]{:S(2)}) collective-permute-start(f32[2,9,36,10]{2,0,3,1:T(2,128)S(1)} %pad_maximum_fusion.11), channel_id=1, source_target_pairs={{2,0},{4,2},{6,4},{3,1},{5,3},{7,5},{10,8},{12,10},{14,12},{11,9},... | collective-permute-start | bytes 77768 | tf_op jit(solution)/shard_map/ppermute | solution.py:24
  303.6 18.3 %collective-permute-start.10 = (f32[2,9,36,10]{2,0,3,1:T(2,128)S(1)}, f32[2,9,36,10]{2,0,3,1:T(2,128)}, u32[]{:S(2)}, u32[]{:S(2)}) collective-permute-start(f32[2,9,36,10]{2,0,3,1:T(2,128)S(1)} %pad_maximum_fusion.11), channel_id=1, source_target_pairs={{0,2},{2,4},{4,6},{1,3},{3,5},{5,7},{8,10},{10,12},{12,14},{9,11},... | collective-permute-start | bytes 77768 | tf_op jit(solution)/shard_map/ppermute | solution.py:22
  314.1 13.8 %copy-start.8 = (bf16[2,3,36,10,128]{4,3,2,1,0:T(8,128)(2,1)S(1)}, bf16[2,3,36,10,128]{4,3,2,1,0:T(8,128)(2,1)}, u32[]{:S(2)}) copy-start(bf16[2,3,36,10,128]{4,3,2,1,0:T(8,128)(2,1)} %copy-done.7) | copy-start | bytes 1658884
  314.1 13.8 %copy-start.10 = (bf16[2,3,36,10,128]{4,3,2,1,0:T(8,128)(2,1)S(1)}, bf16[2,3,36,10,128]{4,3,2,1,0:T(8,128)(2,1)}, u32[]{:S(2)}) copy-start(bf16[2,3,36,10,128]{4,3,2,1,0:T(8,128)(2,1)} %copy-done.9) | copy-start | bytes 1658884
  314.1 13.9 %copy-start.12 = (bf16[3,36,10,128]{3,2,1,0:T(8,128)(2,1)S(1)}, bf16[3,36,10,128]{3,2,1,0:T(8,128)(2,1)}, u32[]{:S(2)}) copy-start(bf16[3,36,10,128]{3,2,1,0:T(8,128)(2,1)} %copy-done.11) | copy-start | bytes 829444
  314.1 13.9 %copy-start.14 = (bf16[1,3,36,10,128]{4,3,2,1,0:T(8,128)(2,1)S(1)}, bf16[1,3,36,10,128]{4,3,2,1,0:T(8,128)(2,1)}, u32[]{:S(2)}) copy-start(bf16[1,3,36,10,128]{4,3,2,1,0:T(8,128)(2,1)} %copy-done.13) | copy-start | bytes 829444
  333.7 13.1 %copy-start.31 = (bf16[540,128]{1,0:T(8,128)(2,1)S(1)}, bf16[540,128]{1,0:T(8,128)(2,1)}, u32[]{:S(2)}) copy-start(bf16[540,128]{1,0:T(8,128)(2,1)} %reshape.372) | copy-start | bytes 414724
  333.7 13.1 %copy-start.36 = (s32[9720]{0:T(1024)S(1)}, s32[9720]{0:T(1024)}, u32[]{:S(2)}) copy-start(s32[9720]{0:T(1024)} %select_n.98) | copy-start | bytes 116644
  333.7 13.1 %copy-start.37 = (pred[9720]{0:T(1024)(128)(4,1)S(1)}, pred[9720]{0:T(1024)(128)(4,1)}, u32[]{:S(2)}) copy-start(pred[9720]{0:T(1024)(128)(4,1)} %and.214) | copy-start | bytes 29164
  333.7 13.1 %copy-start.43 = (s32[540]{0:T(1024)S(1)}, s32[540]{0:T(1024)}, u32[]{:S(2)}) copy-start(s32[540]{0:T(1024)} %select_n.101) | copy-start | bytes 6484
  333.7 13.1 %copy-start.44 = (pred[540]{0:T(1024)(128)(4,1)S(1)}, pred[540]{0:T(1024)(128)(4,1)}, u32[]{:S(2)}) copy-start(pred[540]{0:T(1024)(128)(4,1)} %and.220) | copy-start | bytes 1624
  346.8 17.3 %copy-start.26 = (bf16[540,128]{1,0:T(8,128)(2,1)S(1)}, bf16[540,128]{1,0:T(8,128)(2,1)}, u32[]{:S(2)}) copy-start(bf16[540,128]{1,0:T(8,128)(2,1)} %reshape.373) | copy-start | bytes 414724
  376.3 16.1 %copy-start.32 = (bf16[540,128]{1,0:T(8,128)(2,1)S(1)}, bf16[540,128]{1,0:T(8,128)(2,1)}, u32[]{:S(2)}) copy-start(bf16[540,128]{1,0:T(8,128)(2,1)} %reshape.370) | copy-start | bytes 414724
  376.3 16.1 %copy-start.41 = (s32[540]{0:T(1024)S(1)}, s32[540]{0:T(1024)}, u32[]{:S(2)}) copy-start(s32[540]{0:T(1024)} %select_n.96) | copy-start | bytes 6484
  376.3 16.1 %copy-start.45 = (pred[540]{0:T(1024)(128)(4,1)S(1)}, pred[540]{0:T(1024)(128)(4,1)}, u32[]{:S(2)}) copy-start(pred[540]{0:T(1024)(128)(4,1)} %and.216) | copy-start | bytes 1624
  392.4 17.1 %copy-start.27 = (bf16[540,128]{1,0:T(8,128)(2,1)S(1)}, bf16[540,128]{1,0:T(8,128)(2,1)}, u32[]{:S(2)}) copy-start(bf16[540,128]{1,0:T(8,128)(2,1)} %reshape.371) | copy-start | bytes 414724
  421.4 16.1 %copy-start.22 = (bf16[9720,128,1,1]{1,0,2,3:T(8,128)(2,1)S(1)}, bf16[9720,128,1,1]{1,0,2,3:T(8,128)(2,1)}, u32[]{:S(2)}) copy-start(bf16[9720,128,1,1]{1,0,2,3:T(8,128)(2,1)} %reshape.375) | copy-start | bytes 7464964
  469.5 16.1 %copy-start.21 = (bf16[9720,128,1,1]{1,0,2,3:T(8,128)(2,1)S(1)}, bf16[9720,128,1,1]{1,0,2,3:T(8,128)(2,1)}, u32[]{:S(2)}) copy-start(bf16[9720,128,1,1]{1,0,2,3:T(8,128)(2,1)} %reshape.376) | copy-start | bytes 7464964
  485.6 15.9 %copy-start.1 = (bf16[256,1536]{1,0:T(8,128)(2,1)S(1)}, bf16[256,1536]{1,0:T(8,128)(2,1)}, u32[]{:S(2)}) copy-start(bf16[256,1536]{1,0:T(8,128)(2,1)} %param.10) | copy-start | bytes 2359300
  (13 other events, 90.1 us)
Sparse Core Ops, SparseCore 0:
  34.3 15.9 reduce-scatter.6
Sparse Core Ops, SparseCore 1:
  321.4 57.4 reduce-scatter.4
where the time goes:
time: 520 us; the launch traced here: 509 us
  local copies, waits for them, and re-layouts  247 us (48%)
  matrix products  171 us (33%)
  starting transfers between devices  37.1 us (7%)
  other arithmetic  27.3 us (5%)
  between operations  16.7 us (3%)
  blocking collectives  8.65 us (2%)
    dot_general x9, matrix products, product_nt(): lax.dot_general(left, right, (((1,), (1,)), ((), ())), preferred_element_...  105 us
    dot_general x4, local copies, waits for them, and re-layouts, product_tn(): lax.dot_general(left, right, (((0,), (0,)), ((), ())), preferred_element_...  64.3 us
    unnamed x102, local copies, waits for them, and re-layouts  35.3 us
    dot_general x2, local copies, waits for them, and re-layouts, attend_backward(): jnp.dot(dscore, key_band, preferred_element_type=jnp.float32)  32.2 us
    ppermute x6, starting transfers between devices, extended(): lax.ppermute(tail, axis, [(i, (i + 1) % count) for i in range(ends)])  29.4 us
    dot_general x5, matrix products, product_tn(): lax.dot_general(left, right, (((0,), (0,)), ((), ())), preferred_element_...  28.2 us
    dot_general x2, matrix products, attend_forward(): jnp.dot(expos.astype(jnp.bfloat16), value_band, preferred_element_type=jn...  21.5 us
    dot_general x2, matrix products, attend_backward(): jnp.dot(dscore, key_band, preferred_element_type=jnp.float32)  14.1 us
  transfers between devices with their start and end apart: 14, of which 1 were waited for; matrix products, arithmetic and copies ran while one was open for 84% of the time, Pallas kernels for 0%

commit v1 on v0

v1 whole, which is shorter than its diff:
```python
import functools
import math

import jax
import jax.numpy as jnp
from jax import lax
from jax.experimental import pallas as pl
from jax.experimental.pallas import tpu as pltpu
from jax.sharding import PartitionSpec as P

TH = 9
FAR = 1e30
LOG2E = 1.4426950408889634


def round_up(value, step):
    return -(-value // step) * step


def dot_nt(left, right):
    return lax.dot_general(
        left, right, (((1,), (1,)), ((), ())), preferred_element_type=jnp.float32
    )


def gather_tiles(pieces, dests, sems, block):
    copies = []
    index = 0
    for piece in pieces:
        for which, dest in enumerate(dests):
            copies.append((piece.at[which], dest))
    started = []
    for index, (source, dest) in enumerate(copies):
        slot = index // len(dests)
        copy = pltpu.make_async_copy(
            source, dest.at[:, slot * block : (slot + 1) * block, :], sems.at[index]
        )
        copy.start()
        started.append(copy)
    return started


def split_pieces(own, near, far):
    views = [own]
    views += list(near)
    for pair in far:
        views += [pair.at[0], pair.at[1]]
    return views


def query_kernel(
    q_ref, g_ref, bias_ref, own, t_prev, t_next, w_prev, w_next, c_prev, c_next,
    att_ref, gq_ref, stats_ref,
    k_all, v_all, s_buf, top, tot, out, grad, sems,
    *, tiles, block, wide, chunk, scale,
):
    per = wide // chunk
    depth = q_ref.shape[-1]
    fill = jnp.zeros((tiles, wide - 9 * block, depth), jnp.bfloat16)
    k_all[:, 9 * block :, :] = fill
    v_all[:, 9 * block :, :] = fill
    pieces = split_pieces(own, (t_prev, t_next, w_prev, w_next), (c_prev, c_next))
    for copy in gather_tiles(pieces, (k_all, v_all), sems, block):
        copy.wait()

    @pl.loop(0, tiles)
    def _(tile):
        low = jnp.maximum(tile - 1, 0) * per
        high = (jnp.minimum(tile + 1, tiles - 1) + 1) * per
        top[...] = jnp.full(top.shape, -3e38, jnp.float32)
        tot[...] = jnp.zeros(tot.shape, jnp.float32)
        out[...] = jnp.zeros(out.shape, jnp.float32)
        grad[...] = jnp.zeros(grad.shape, jnp.float32)

        @pl.loop(low, high)
        def _(step):
            row = step // per
            start = pl.multiple_of((step % per) * chunk, chunk)
            keys = k_all[row, pl.ds(start, chunk), :]
            scores = dot_nt(q_ref[tile], keys) * (scale * LOG2E)
            scores = scores + bias_ref[row, :, pl.ds(start, chunk)]
            s_buf[step - low] = scores
            best = top[...]
            for lane in range(0, chunk, 128):
                best = jnp.maximum(best, scores[:, lane : lane + 128])
            top[...] = best

        peak = jnp.max(top[...], axis=1, keepdims=True)

        @pl.loop(low, high)
        def _(step):
            row = step // per
            start = pl.multiple_of((step % per) * chunk, chunk)
            expos = jnp.exp2(s_buf[step - low] - peak)
            s_buf[step - low] = expos
            part = tot[...]
            for lane in range(0, chunk, 128):
                part = part + expos[:, lane : lane + 128]
            tot[...] = part
            out[...] += jnp.dot(
                expos.astype(jnp.bfloat16),
                v_all[row, pl.ds(start, chunk), :],
                preferred_element_type=jnp.float32,
            )

        total = jnp.sum(tot[...], axis=1, keepdims=True)
        attended = (out[...] / total).astype(jnp.bfloat16)
        att_ref[tile] = attended
        delta = jnp.sum(
            g_ref[tile].astype(jnp.float32) * attended.astype(jnp.float32), axis=1, keepdims=True
        )
        lanes = lax.broadcasted_iota(jnp.int32, (block, 128), 1)
        stats_ref[tile] = jnp.where(lanes == 0, peak + jnp.log2(total), delta)

        @pl.loop(low, high)
        def _(step):
            row = step // per
            start = pl.multiple_of((step % per) * chunk, chunk)
            dprob = dot_nt(g_ref[tile], v_all[row, pl.ds(start, chunk), :])
            dscore = (s_buf[step - low] * (dprob - delta)).astype(jnp.bfloat16)
            grad[...] += jnp.dot(
                dscore, k_all[row, pl.ds(start, chunk), :], preferred_element_type=jnp.float32
            )

        gq_ref[tile] = (grad[...] * (scale / total)).astype(jnp.bfloat16)


def key_kernel(
    k_ref, v_ref, live_ref, stats_ref, own, t_prev, t_next, w_prev, w_next, c_prev, c_next,
    gk_ref, gv_ref,
    q_all, g_all, grad_k, grad_v, sems,
    *, tiles, block, wide, chunk, scale,
):
    per = wide // chunk
    depth = k_ref.shape[-1]
    fill = jnp.zeros((tiles, wide - 9 * block, depth), jnp.bfloat16)
    q_all[:, 9 * block :, :] = fill
    g_all[:, 9 * block :, :] = fill
    pieces = split_pieces(own, (t_prev, t_next, w_prev, w_next), (c_prev, c_next))
    for copy in gather_tiles(pieces, (q_all, g_all), sems, block):
        copy.wait()

    @pl.loop(0, tiles)
    def _(tile):
        low = jnp.maximum(tile - 1, 0) * per
        high = (jnp.minimum(tile + 1, tiles - 1) + 1) * per
        grad_k[...] = jnp.zeros(grad_k.shape, jnp.float32)
        grad_v[...] = jnp.zeros(grad_v.shape, jnp.float32)

        @pl.loop(low, high)
        def _(step):
            row = step // per
            start = pl.multiple_of((step % per) * chunk, chunk)
            queries = q_all[row, pl.ds(start, chunk), :]
            grads = g_all[row, pl.ds(start, chunk), :]
            lse = stats_ref[row, 0:1, pl.ds(start, chunk)]
            delta = stats_ref[row, 1:2, pl.ds(start, chunk)]
            probs = jnp.exp2(dot_nt(k_ref[tile], queries) * (scale * LOG2E) - lse)
            grad_v[...] += jnp.dot(
                probs.astype(jnp.bfloat16), grads, preferred_element_type=jnp.float32
            )
            dscore = probs * (dot_nt(v_ref[tile], grads) - delta)
            grad_k[...] += jnp.dot(
                dscore.astype(jnp.bfloat16), queries, preferred_element_type=jnp.float32
            )

        live = live_ref[tile] > 0
        gk_ref[tile] = jnp.where(live, grad_k[...] * scale, 0.0).astype(jnp.bfloat16)
        gv_ref[tile] = jnp.where(live, grad_v[...], 0.0).astype(jnp.bfloat16)


def shift(cells, axis, forward):
    count = lax.axis_size(axis)
    if forward:
        pairs = [(i, i + 1) for i in range(count - 1)]
    else:
        pairs = [(i + 1, i) for i in range(count - 1)]
    return lax.ppermute(cells, axis, pairs)


def neighbours(cells):
    t_prev = shift(cells, "tm", True)
    t_next = shift(cells, "tm", False)
    w_prev = shift(cells, "width", True)
    w_next = shift(cells, "width", False)
    pair = jnp.stack([t_prev, t_next])
    return (
        cells, t_prev, t_next, w_prev, w_next,
        shift(pair, "width", True), shift(pair, "width", False),
    )


def lay_out(cells, block, tile_rows):
    frames, columns, rows, depth = cells.shape
    tiles = rows // tile_rows
    cells = cells.reshape(frames * columns, tiles, tile_rows, depth).transpose(1, 0, 2, 3)
    cells = cells.reshape(tiles, frames * columns * tile_rows, depth)
    return jnp.pad(cells, ((0, 0), (0, block - cells.shape[1]), (0, 0)))


def lay_back(cells, frames, columns, tile_rows):
    tiles, _, depth = cells.shape
    count = frames * columns
    cells = cells[:, : count * tile_rows].reshape(tiles, count, tile_rows, depth)
    return cells.transpose(1, 0, 2, 3).reshape(frames, columns, tiles * tile_rows, depth)


def shards(query_heads, key_heads, value_heads, row_valid, out_weight, grad_mixed):
    frames, rows, columns, depth = query_heads.shape
    scale = 1.0 / math.sqrt(depth)
    tiles = rows // TH
    count = frames * columns * TH
    block = round_up(count, 16)
    wide = round_up(9 * block, 256)
    chunk = wide // 2
    swap = (0, 2, 1, 3)
    query = lay_out(query_heads.transpose(swap), block, TH)
    key = lay_out(key_heads.transpose(swap), block, TH)
    value = lay_out(value_heads.transpose(swap), block, TH)
    grad_in = grad_mixed.transpose(swap)

    t_index, w_index = lax.axis_index("tm"), lax.axis_index("width")
    t_back, t_ahead = t_index > 0, t_index < lax.axis_size("tm") - 1
    w_back, w_ahead = w_index > 0, w_index < lax.axis_size("width") - 1
    exists = jnp.stack([
        t_index >= 0, t_back, t_ahead, w_back, w_ahead,
        t_back & w_back, t_ahead & w_back, t_back & w_ahead, t_ahead & w_ahead,
    ])
    live = jnp.broadcast_to(
        (row_valid > 0).reshape(tiles, 1, TH), (tiles, frames * columns, TH)
    ).reshape(tiles, count)
    live = jnp.pad(live, ((0, 0), (0, block - count)))
    wide_live = (live[:, None, :] & exists[None, :, None]).reshape(tiles, 9 * block)
    wide_live = jnp.pad(wide_live, ((0, 0), (0, wide - 9 * block)))
    bias = jnp.where(wide_live, 0.0, -FAR).astype(jnp.float32)[:, None, :]

    key_value = neighbours(jnp.stack([key, value]))
    grad_heads = lax.dot_general(
        grad_in, out_weight, (((3,), (1,)), ((), ())), preferred_element_type=jnp.float32
    )
    grad_own = lax.psum_scatter(
        grad_heads.astype(jnp.bfloat16), "head", scatter_dimension=3, tiled=True
    )
    grad_own = lay_out(grad_own, block, TH)
    query_grad = neighbours(jnp.stack([query, grad_own]))

    pairs = tiles * 3 - 2
    work = pairs * block * wide
    in_vmem = pl.BlockSpec(memory_space=pltpu.VMEM)
    in_any = pl.BlockSpec(memory_space=pl.ANY)
    params = dict(tiles=tiles, block=block, wide=wide, chunk=chunk, scale=scale)
    flat = jax.ShapeDtypeStruct((tiles, block, depth), jnp.bfloat16)
    wide_bf16 = pltpu.VMEM((tiles, wide, depth), jnp.bfloat16)
    acc = pltpu.VMEM((block, depth), jnp.float32)
    lane_acc = pltpu.VMEM((block, 128), jnp.float32)
    cost = pl.CostEstimate(
        flops=16 * work * depth, transcendentals=work, bytes_accessed=4 * tiles * wide * depth
    )
    attended, grad_query, stats = pl.pallas_call(
        functools.partial(query_kernel, **params),
        out_shape=(flat, flat, jax.ShapeDtypeStruct((tiles, block, 128), jnp.float32)),
        in_specs=[in_vmem] * 3 + [in_any] * 7,
        out_specs=(in_vmem, in_vmem, in_vmem),
        scratch_shapes=[
            wide_bf16, wide_bf16,
            pltpu.VMEM((min(3, tiles) * (wide // chunk), block, chunk), jnp.float32),
            lane_acc, lane_acc, acc, acc,
            pltpu.SemaphoreType.DMA((18,)),
        ],
        compiler_params=pltpu.CompilerParams(vmem_limit_bytes=50 << 20),
        cost_estimate=cost,
        name="query_side",
    )(query, grad_own, bias, *key_value)

    stats_own = stats[:, :, :2].transpose(0, 2, 1)
    near = neighbours(stats_own)
    joined = jnp.stack(list(near[:5]) + [near[5][0], near[5][1], near[6][0], near[6][1]], axis=2)
    blank = jnp.array([FAR, 0.0], jnp.float32)[None, :, None, None]
    joined = jnp.where(exists[None, None, :, None], joined, blank).reshape(tiles, 2, 9 * block)
    tail = jnp.broadcast_to(blank[..., 0], (tiles, 2, wide - 9 * block))
    stats_wide = jnp.concatenate([joined, tail], axis=2)

    attended = lay_back(attended, frames, columns, TH)
    other = lax.ppermute(attended, "head", [(0, 1), (1, 0)])
    first = lax.axis_index("head") == 0
    heads_all = jnp.concatenate(
        [jnp.where(first, attended, other), jnp.where(first, other, attended)], axis=3
    )
    mixed = lax.dot_general(
        heads_all, out_weight, (((3,), (0,)), ((), ())), preferred_element_type=jnp.float32
    ).astype(jnp.bfloat16)
    grad_weight = lax.psum_scatter(
        lax.dot_general(
            heads_all, grad_in, (((0, 1, 2), (0, 1, 2)), ((), ())),
            preferred_element_type=jnp.float32,
        ),
        ("tm", "width"), scatter_dimension=0, tiled=True,
    )

    live_rows = live.astype(jnp.float32)[:, :, None]
    grad_key, grad_value = pl.pallas_call(
        functools.partial(key_kernel, **params),
        out_shape=(flat, flat),
        in_specs=[in_vmem] * 4 + [in_any] * 7,
        out_specs=(in_vmem, in_vmem),
        scratch_shapes=[wide_bf16, wide_bf16, acc, acc, pltpu.SemaphoreType.DMA((18,))],
        compiler_params=pltpu.CompilerParams(vmem_limit_bytes=50 << 20),
        cost_estimate=cost,
        name="key_side",
    )(key, value, live_rows, stats_wide, *query_grad)

    back = lambda cells: lay_back(cells, frames, columns, TH).transpose(swap)
    return (mixed.transpose(swap), back(grad_query), back(grad_key), back(grad_value), grad_weight)


def solution(mesh):
    split = P("tm", None, "width", "head")
    return jax.shard_map(
        shards,
        mesh=mesh,
        in_specs=(split, split, split, P(), P(None, "head"), split),
        out_specs=(split, split, split, split, P(("tm", "width"), "head")),
        check_vma=False,
    )
```

time: 520 us -> 245 us (0.47); the launches traced: 509 us -> 244 us
  local copies, waits for them, and re-layouts: 247 us -> 55.8 us
  matrix products: 171 us -> 11.7 us
  waiting for transfers between devices: 1.18 us -> 61.1 us
  Pallas kernels: 0 us -> 49.9 us
  other arithmetic: 27.3 us -> 4.9 us
  blocking collectives: 8.65 us -> 0 us
  starting transfers between devices: 37.1 us -> 45.4 us
    dot_general x19 -> x3, matrix products: 171 us -> 11.7 us  [the longest x1 4.45 us: shards(): lax.dot_general(heads_all, grad_in, (((0, 1, 2), (0, 1, 2)), ((), ())), p...]
    dot_general x6 -> x0, local copies, waits for them, and re-layouts: 96.5 us -> none  [the longest x4 64.3 us: product_tn(): lax.dot_general(left, right, (((0,), (0,)), ((), ())), preferred_element_...]
    pallas_call x0 -> x2, Pallas kernels: none -> 49.9 us  [the longest x1 29.2 us: shards(): pl.pallas_call(functools.partial(query_kernel, **params), out_shape=(flat...]
    reduce_scatter x1, waiting for transfers between devices: 0.01 us -> 30.7 us  [shards(): lax.psum_scatter(lax.dot_general(heads_all, grad_in, (((0, 1, 2), (0, 1,...]
    reshape x14, local copies, waits for them, and re-layouts: 33.5 us -> 2.85 us  [the longest x4 1.38 us: lay_out(): cells.reshape(frames * columns, tiles, tile_rows, depth)]
    ppermute x12 -> x19, waiting for transfers between devices: 0.03 us -> 21.3 us  [the longest x18 21.3 us: shift(): return lax.ppermute(cells, axis, pairs)]
    slice x19 -> x6, local copies, waits for them, and re-layouts: 24.2 us -> 3.37 us  [the longest x4 3.36 us: lay_back(): cells = cells[:, :count * tile_rows].reshape(tiles, count, tile_rows, depth)]
    another operation x13 -> x5, local copies, waits for them, and re-layouts: 25.7 us -> 7.44 us  [the longest x3 6.38 us: shards(): jnp.stack(list(near[:5]) + [near[5][0], near[5][1], near[6][0], near[6][1...]
  transfers between devices with their start and end apart: 14 -> 21, of which waited for: 1 -> 6; matrix products, arithmetic and copies ran while one was open for 84% -> 22% of each run, Pallas kernels for 0% -> 21%
where the time goes in v1:
time: 245 us; the launch traced here: 244 us
  waiting for transfers between devices  61.1 us (25%)
  local copies, waits for them, and re-layouts  55.8 us (23%)
  Pallas kernels  49.9 us (20%)
  starting transfers between devices  45.4 us (19%)
  between operations  14.7 us (6%)
  matrix products  11.7 us (5%)
  other arithmetic  4.9 us (2%)
    ppermute x18, starting transfers between devices, shift(): return lax.ppermute(cells, axis, pairs)  44.8 us
    unnamed x57, local copies, waits for them, and re-layouts  36.1 us
    reduce_scatter x1, waiting for transfers between devices, shards(): lax.psum_scatter(lax.dot_general(heads_all, grad_in, (((0, 1, 2), (0, 1,...  30.7 us
    pallas_call x1, Pallas kernels, shards(): pl.pallas_call(functools.partial(query_kernel, **params), out_shape=(flat...  29.2 us
    ppermute x18, waiting for transfers between devices, shift(): return lax.ppermute(cells, axis, pairs)  21.3 us
    pallas_call x1, Pallas kernels, shards(): pl.pallas_call(functools.partial(key_kernel, **params), out_shape=(flat,...  20.8 us
    unnamed x3, waiting for transfers between devices  9.1 us
    another operation x3, local copies, waits for them, and re-layouts, shards(): jnp.stack(list(near[:5]) + [near[5][0], near[5][1], near[6][0], near[6][1...  6.38 us
  transfers between devices with their start and end apart: 21, of which 6 were waited for; matrix products, arithmetic and copies ran while one was open for 22% of the time, Pallas kernels for 21%

profile of v1, /device:TPU:0, one launch (start us, length us, event | category | flops | bytes accessed | tf_op | source)
XLA Modules:
  0.0 243.6 jit_solution(13561990046214791504)
XLA Ops:
  7.2 1.1 copy-done
  8.3 3.2 %fusion.8 = bf16[3,10,36,256]{3,2,1,0:T(8,128)(2,1)S(1)} fusion(bf16[3,36,10,1536]{3,1,2,0:T(8,128)(2,1)} %param.12, bf16[256,1536]{1,0:T(8,128)(2,1)S(1)} %copy-done), kind=kOutput, calls=%fused_computation.7 | convolution fusion | flops 849623040 | bytes 4657152 | tf_op jit(solution)/shard_map/dot_general | solution.py:238
  11.6 3.8 %copy.140 = bf16[3,10,36,256]{2,1,0,3:T(8,128)(2,1)} copy(bf16[3,10,36,256]{3,2,1,0:T(8,128)(2,1)S(1)} %fusion.8) | data formatting | bytes 1105920
  15.4 4.5 %reshape.98 = bf16[256,1080]{1,0:T(8,128)(2,1)} reshape(bf16[256,3,10,36]{3,2,1,0:T(8,128)(2,1)} %bitcast.117) | data formatting | bytes 1105920
  21.5 5.0 %collective-permute-start = (bf16[2,4,272,128]{3,2,1,0:T(8,128)(2,1)S(1)}, bf16[2,4,272,128]{3,2,1,0:T(8,128)(2,1)S(1)}, u32[]{:S(2)}, u32[]{:S(2)}) collective-permute-start(bf16[2,4,272,128]{3,2,1,0:T(8,128)(2,1)S(1)} %pad_maximum_fusion.3.own), channel_id=1, source_target_pairs={{0,8},{8,16},{16,24},{1,9},{9,17},{17,25},{2,10},{10,18},{18,26},{... | collective-permute-start | bytes 1671176 | tf_op jit(solution)/shard_map/ppermute | solution.py:178
  26.5 1.3 collective-permute-start.1
  27.8 1.1 reshape.94
  29.0 9.1 %reduce-scatter.7.cloned.1.call-done = bf16[128,1080]{1,0:T(8,128)(2,1)} async-done(((bf16[256,1080]{1,0:T(8,128)(2,1)}), bf16[128,1080]{1,0:T(8,128)(2,1)}) %reduce-scatter.7.cloned.1.call-update) | async-done | bytes 276496
  38.1 3.3 %reshape.99 = bf16[128,3,10,36]{3,2,1,0:T(8,128)(2,1)} reshape(bf16[128,1080]{1,0:T(8,128)(2,1)} %reduce-scatter.7.cloned.1.call-done) | data formatting | bytes 552960
  41.4 2.4 copy.141
  45.2 3.4 %collective-permute-start.13 = (bf16[2,4,272,128]{3,2,1,0:T(8,128)(2,1)S(1)}, bf16[2,4,272,128]{3,2,1,0:T(8,128)(2,1)S(1)}, u32[]{:S(2)}, u32[]{:S(2)}) collective-permute-start(bf16[2,4,272,128]{3,2,1,0:T(8,128)(2,1)S(1)} %pad_maximum_fusion.4.own), channel_id=1, source_target_pairs={{0,8},{8,16},{16,24},{1,9},{9,17},{17,25},{2,10},{10,18},{18,26},{... | collective-permute-start | bytes 1671176 | tf_op jit(solution)/shard_map/ppermute | solution.py:178
  48.6 2.2 collective-permute-start.2
  50.8 1.3 collective-permute-start.3
  52.9 2.3 pad_maximum_fusion
  55.2 4.8 %collective-permute-start.4 = (bf16[2,2,4,272,128]{4,3,2,1,0:T(8,128)(2,1)}, bf16[2,2,4,272,128]{4,3,2,1,0:T(8,128)(2,1)}, u32[]{:S(2)}, u32[]{:S(2)}) collective-permute-start(bf16[2,2,4,272,128]{4,3,2,1,0:T(8,128)(2,1)} %pad_maximum_fusion), channel_id=1, source_target_pairs={{0,2},{2,4},{4,6},{1,3},{3,5},{5,7},{8,10},{10,12},{12,14},{9,11},... | collective-permute-start | bytes 3342344 | tf_op jit(solution)/shard_map/ppermute | solution.py:178
  60.0 1.3 collective-permute-start.5
  61.3 1.3 collective-permute-start.14
  62.7 1.1 copy.122.live_ref
  63.8 14.6 %collective-permute-done.14.t_next = bf16[2,4,272,128]{3,2,1,0:T(8,128)(2,1)S(1)} collective-permute-done((bf16[2,4,272,128]{3,2,1,0:T(8,128)(2,1)S(1)}, bf16[2,4,272,128]{3,2,1,0:T(8,128)(2,1)S(1)}, u32[]{:S(2)}, u32[]{:S(2)}) %collective-permute-start.14) | collective-permute-done | bytes 557088 | tf_op jit(solution)/shard_map/ppermute | solution.py:178
  78.4 2.9 %collective-permute-start.15 = (bf16[2,4,272,128]{3,2,1,0:T(8,128)(2,1)S(1)}, bf16[2,4,272,128]{3,2,1,0:T(8,128)(2,1)}, u32[]{:S(2)}, u32[]{:S(2)}) collective-permute-start(bf16[2,4,272,128]{3,2,1,0:T(8,128)(2,1)S(1)} %pad_maximum_fusion.4.own), channel_id=1, source_target_pairs={{0,2},{2,4},{4,6},{1,3},{3,5},{5,7},{8,10},{10,12},{12,14},{9,11},... | collective-permute-start | bytes 1671176 | tf_op jit(solution)/shard_map/ppermute | solution.py:178
  81.3 1.2 pad_maximum_fusion.1
  82.5 1.3 collective-permute-start.16
  83.8 4.8 %collective-permute-start.17 = (bf16[2,2,4,272,128]{4,3,2,1,0:T(8,128)(2,1)}, bf16[2,2,4,272,128]{4,3,2,1,0:T(8,128)(2,1)}, u32[]{:S(2)}, u32[]{:S(2)}) collective-permute-start(bf16[2,2,4,272,128]{4,3,2,1,0:T(8,128)(2,1)} %pad_maximum_fusion.1), channel_id=1, source_target_pairs={{0,2},{2,4},{4,6},{1,3},{3,5},{5,7},{8,10},{10,12},{12,14},{9,11},... | collective-permute-start | bytes 3342344 | tf_op jit(solution)/shard_map/ppermute | solution.py:178
  88.6 1.3 collective-permute-start.18
  89.9 1.0 copy-done.3
  90.9 1.1 copy-done.5
  93.9 29.2 %query_side.1 = (bf16[4,272,128]{2,1,0:T(8,128)(2,1)S(1)}, bf16[4,272,128]{2,1,0:T(8,128)(2,1)S(1)}, f32[4,272,128]{2,1,0:T(8,128)S(1)}) custom-call(bf16[4,272,128]{2,1,0:T(8,128)(2,1)S(1)} %copy-done.8, bf16[4,272,128]{2,1,0:T(8,128)(2,1)S(1)} %copy-done.7, f32[4,1,2560]{2,1,0:T(1,128)S(1)} %broadcast_in_dim.52.bias_ref, ...), custom_call_target="tpu_custom_call" | custom-call | flops 14260633600 | bytes 5242880 | tf_op jit(solution)/shard_map/query_side/pallas_call | solution.py:259
  125.3 1.3 copy.109
  126.6 3.3 %collective-permute-start.7 = (f32[4,2,272]{2,0,1:T(4,128)S(1)}, f32[4,2,272]{2,0,1:T(4,128)S(1)}, u32[]{:S(2)}, u32[]{:S(2)}) collective-permute-start(f32[4,2,272]{2,0,1:T(4,128)S(1)} %copy.109), channel_id=1, source_target_pairs={{0,8},{8,16},{16,24},{1,9},{9,17},{17,25},{2,10},{10,18},{18,26},{... | collective-permute-start | bytes 26120 | tf_op jit(solution)/shard_map/ppermute | solution.py:178
  130.8 1.1 copy.102
  132.8 1.1 copy.107
  134.8 1.3 collective-permute-start.8
  137.3 3.2 %collective-permute-done.8 = f32[4,2,272]{2,0,1:T(4,128)S(1)} collective-permute-done((f32[4,2,272]{2,0,1:T(4,128)S(1)}, f32[4,2,272]{2,0,1:T(4,128)S(1)}, u32[]{:S(2)}, u32[]{:S(2)}) %collective-permute-start.8) | collective-permute-done | bytes 8736 | tf_op jit(solution)/shard_map/ppermute | solution.py:178
  140.5 2.0 collective-permute-start.9
  143.6 1.3 collective-permute-start.10
  146.0 3.2 %collective-permute-done.10 = f32[4,2,272]{2,0,1:T(4,128)S(1)} collective-permute-done((f32[4,2,272]{2,0,1:T(4,128)S(1)}, f32[4,2,272]{2,0,1:T(4,128)S(1)}, u32[]{:S(2)}, u32[]{:S(2)}) %collective-permute-start.10) | collective-permute-done | bytes 8736 | tf_op jit(solution)/shard_map/ppermute | solution.py:178
  149.1 4.6 %collective-permute-start.11 = (f32[2,4,2,272]{3,1,2,0:T(4,128)S(1)}, f32[2,4,2,272]{3,1,2,0:T(4,128)S(1)}, u32[]{:S(2)}, u32[]{:S(2)}) collective-permute-start(f32[2,4,2,272]{3,1,2,0:T(4,128)S(1)} %pad_maximum_fusion.8), channel_id=1, source_target_pairs={{0,2},{2,4},{4,6},{1,3},{3,5},{5,7},{8,10},{10,12},{12,14},{9,11},... | collective-permute-start | bytes 52232 | tf_op jit(solution)/shard_map/ppermute | solution.py:178
  154.8 1.5 collective-permute-start.12
  156.5 1.1 copy.145
  158.4 1.1 copy.146
  160.3 1.9 bitcast_dynamic-update-slice_fusion.3
  162.2 1.9 bitcast_dynamic-update-slice_fusion.2
  165.2 5.4 %copy.121 = f32[4,2,9,272]{3,2,1,0:T(8,128)S(1)} copy(f32[4,2,9,272]{1,3,0,2:T(8,128)} %bitcast_dynamic-update-slice_fusion.1) | data formatting | bytes 156672 | tf_op jit(solution)/shard_map/stack | solution.py:277
  172.6 4.4 %fusion.5 = f32[256,1536]{1,0:T(8,128)} fusion(bf16[3,36,10,1536]{3,1,2,0:T(8,128)(2,1)} %param.12, bf16[3,10,36,128]{3,2,1,0:T(8,128)(2,1)S(1)} %get-tuple-element.31, bf16[3,10,36,128]{3,2,1,0:T(8,128)(2,1)S(1)} %get-tuple-element.30), kind=kOutput, calls=%fused_computation.6 | convolution fusion | flops 850452480 | bytes 5443584 | tf_op jit(solution)/shard_map/dot_general | solution.py:293
  177.4 4.0 %fusion.4 = bf16[3,36,10,1536]{3,1,2,0:T(8,128)(2,1)} fusion(bf16[256,1536]{1,0:T(8,128)(2,1)S(1)} %copy-done, bf16[3,10,36,128]{3,2,1,0:T(8,128)(2,1)} %copy-done.13, bf16[3,10,36,128]{3,2,1,0:T(8,128)(2,1)} %copy-done.12), kind=kOutput, calls=%fused_computation.5 | convolution fusion | flops 852111360 | bytes 4657152 | tf_op jit(solution)/shard_map/dot_general | solution.py:289
  181.5 20.8 %key_side.1 = (bf16[4,272,128]{2,1,0:T(8,128)(2,1)S(1)}, bf16[4,272,128]{2,1,0:T(8,128)(2,1)S(1)}) custom-call(bf16[4,272,128]{2,1,0:T(8,128)(2,1)S(1)} %copy-done.6, bf16[4,272,128]{2,1,0:T(8,128)(2,1)S(1)} %get-tuple-element.36.v_ref, f32[4,272,1]{2,1,0:T(8,128)S(1)} %copy-done.1, f32[4,2,2560]{2,1,0:T(2,128)S(1)} %pad_maximum_fusion.7.stats_ref, ...), custom_call_target="tpu_custom_call" | custom-call | flops 14260633600 | bytes 5242880 | tf_op jit(solution)/shard_map/key_side/pallas_call | solution.py:301
  204.0 1.1 copy.125
  206.1 30.7 %reduce-scatter.5.cloned.1.call-done = f32[16,1536]{1,0:T(8,128)} async-done(((f32[256,1536]{1,0:T(8,128)}), f32[16,1536]{1,0:T(8,128)}) %reduce-scatter.5.cloned.1.call-update) | async-done | bytes 98320 | tf_op jit(solution)/shard_map/reduce_scatter | solution.py:292
  (118 shorter events, 22.9 us)
Async XLA Ops:
  7.2 1.1 copy-start
  7.2 30.9 %reduce-scatter.7.cloned.1.call-start = ((), (), s32[]{:S(2)}) async-start(), calls=%async_computation.3 | async-start | bytes 884736
  11.6 8.5 %copy-start.15 = (bf16[3,36,10,128]{3,1,2,0:T(8,128)(2,1)S(1)}, bf16[3,36,10,128]{3,1,2,0:T(8,128)(2,1)}, u32[]{:S(2)}) copy-start(bf16[3,36,10,128]{3,1,2,0:T(8,128)(2,1)} %param.9) | copy-start | bytes 829444
  15.4 4.9 %copy-start.16 = (bf16[3,36,10,128]{3,1,2,0:T(8,128)(2,1)S(1)}, bf16[3,36,10,128]{3,1,2,0:T(8,128)(2,1)}, u32[]{:S(2)}) copy-start(bf16[3,36,10,128]{3,1,2,0:T(8,128)(2,1)} %param.8) | copy-start | bytes 829444
  20.0 216.8 %reduce-scatter.5.cloned.1.call-start = ((), (), s32[]{:S(2)}) async-start(), calls=%async_computation.2 | async-start | bytes 1671168 | tf_op jit(solution)/shard_map/reduce_scatter | solution.py:292
  21.5 29.3 %copy-start.2 = (bf16[2,4,272,128]{3,2,1,0:T(8,128)(2,1)}, bf16[2,4,272,128]{3,2,1,0:T(8,128)(2,1)S(1)}, u32[]{:S(2)}) copy-start(bf16[2,4,272,128]{3,2,1,0:T(8,128)(2,1)S(1)} %pad_maximum_fusion.3.own) | copy-start | bytes 1671172
  21.5 31.3 %collective-permute-start = (bf16[2,4,272,128]{3,2,1,0:T(8,128)(2,1)S(1)}, bf16[2,4,272,128]{3,2,1,0:T(8,128)(2,1)S(1)}, u32[]{:S(2)}, u32[]{:S(2)}) collective-permute-start(bf16[2,4,272,128]{3,2,1,0:T(8,128)(2,1)S(1)} %pad_maximum_fusion.3.own), channel_id=1, source_target_pairs={{0,8},{8,16},{16,24},{1,9},{9,17},{17,25},{2,10},{10,18},{18,26},{... | collective-permute-start | bytes 1671176 | tf_op jit(solution)/shard_map/ppermute | solution.py:178
  26.5 26.4 %collective-permute-start.1 = (bf16[2,4,272,128]{3,2,1,0:T(8,128)(2,1)S(1)}, bf16[2,4,272,128]{3,2,1,0:T(8,128)(2,1)}, u32[]{:S(2)}, u32[]{:S(2)}) collective-permute-start(bf16[2,4,272,128]{3,2,1,0:T(8,128)(2,1)S(1)} %pad_maximum_fusion.3.own), channel_id=1, source_target_pairs={{8,0},{16,8},{24,16},{9,1},{17,9},{25,17},{10,2},{18,10},{26,18},{... | collective-permute-start | bytes 1671176 | tf_op jit(solution)/shard_map/ppermute | solution.py:178
  41.4 11.0 %copy-start.18 = (s32[36]{0:T(128)S(1)}, s32[36]{0:T(128)}, u32[]{:S(2)}) copy-start(s32[36]{0:T(128)} %param.10) | copy-start | bytes 436
  45.2 16.2 %collective-permute-start.13 = (bf16[2,4,272,128]{3,2,1,0:T(8,128)(2,1)S(1)}, bf16[2,4,272,128]{3,2,1,0:T(8,128)(2,1)S(1)}, u32[]{:S(2)}, u32[]{:S(2)}) collective-permute-start(bf16[2,4,272,128]{3,2,1,0:T(8,128)(2,1)S(1)} %pad_maximum_fusion.4.own), channel_id=1, source_target_pairs={{0,8},{8,16},{16,24},{1,9},{9,17},{17,25},{2,10},{10,18},{18,26},{... | collective-permute-start | bytes 1671176 | tf_op jit(solution)/shard_map/ppermute | solution.py:178
  48.6 33.9 %collective-permute-start.2 = (bf16[2,4,272,128]{3,2,1,0:T(8,128)(2,1)S(1)}, bf16[2,4,272,128]{3,2,1,0:T(8,128)(2,1)}, u32[]{:S(2)}, u32[]{:S(2)}) collective-permute-start(bf16[2,4,272,128]{3,2,1,0:T(8,128)(2,1)S(1)} %pad_maximum_fusion.3.own), channel_id=1, source_target_pairs={{0,2},{2,4},{4,6},{1,3},{3,5},{5,7},{8,10},{10,12},{12,14},{9,11},... | collective-permute-start | bytes 1671176 | tf_op jit(solution)/shard_map/ppermute | solution.py:178
  50.8 32.9 %collective-permute-start.3 = (bf16[2,4,272,128]{3,2,1,0:T(8,128)(2,1)S(1)}, bf16[2,4,272,128]{3,2,1,0:T(8,128)(2,1)}, u32[]{:S(2)}, u32[]{:S(2)}) collective-permute-start(bf16[2,4,272,128]{3,2,1,0:T(8,128)(2,1)S(1)} %pad_maximum_fusion.3.own), channel_id=1, source_target_pairs={{2,0},{4,2},{6,4},{3,1},{5,3},{7,5},{10,8},{12,10},{14,12},{11,9},... | collective-permute-start | bytes 1671176 | tf_op jit(solution)/shard_map/ppermute | solution.py:178
  52.8 8.5 %copy-start.4 = (bf16[2,4,272,128]{3,2,1,0:T(8,128)(2,1)}, bf16[2,4,272,128]{3,2,1,0:T(8,128)(2,1)S(1)}, u32[]{:S(2)}) copy-start(bf16[2,4,272,128]{3,2,1,0:T(8,128)(2,1)S(1)} %collective-permute-done.t_prev) | copy-start | bytes 1671172
  55.2 33.4 %collective-permute-start.4 = (bf16[2,2,4,272,128]{4,3,2,1,0:T(8,128)(2,1)}, bf16[2,2,4,272,128]{4,3,2,1,0:T(8,128)(2,1)}, u32[]{:S(2)}, u32[]{:S(2)}) collective-permute-start(bf16[2,2,4,272,128]{4,3,2,1,0:T(8,128)(2,1)} %pad_maximum_fusion), channel_id=1, source_target_pairs={{0,2},{2,4},{4,6},{1,3},{3,5},{5,7},{8,10},{10,12},{12,14},{9,11},... | collective-permute-start | bytes 3342344 | tf_op jit(solution)/shard_map/ppermute | solution.py:178
  60.0 29.8 %collective-permute-start.5 = (bf16[2,2,4,272,128]{4,3,2,1,0:T(8,128)(2,1)}, bf16[2,2,4,272,128]{4,3,2,1,0:T(8,128)(2,1)}, u32[]{:S(2)}, u32[]{:S(2)}) collective-permute-start(bf16[2,2,4,272,128]{4,3,2,1,0:T(8,128)(2,1)} %pad_maximum_fusion), channel_id=1, source_target_pairs={{2,0},{4,2},{6,4},{3,1},{5,3},{7,5},{10,8},{12,10},{14,12},{11,9},... | collective-permute-start | bytes 3342344 | tf_op jit(solution)/shard_map/ppermute | solution.py:178
  61.3 17.1 %collective-permute-start.14 = (bf16[2,4,272,128]{3,2,1,0:T(8,128)(2,1)S(1)}, bf16[2,4,272,128]{3,2,1,0:T(8,128)(2,1)S(1)}, u32[]{:S(2)}, u32[]{:S(2)}) collective-permute-start(bf16[2,4,272,128]{3,2,1,0:T(8,128)(2,1)S(1)} %pad_maximum_fusion.4.own), channel_id=1, source_target_pairs={{8,0},{16,8},{24,16},{9,1},{17,9},{25,17},{10,2},{18,10},{26,18},{... | collective-permute-start | bytes 1671176 | tf_op jit(solution)/shard_map/ppermute | solution.py:178
  78.4 103.0 %collective-permute-start.15 = (bf16[2,4,272,128]{3,2,1,0:T(8,128)(2,1)S(1)}, bf16[2,4,272,128]{3,2,1,0:T(8,128)(2,1)}, u32[]{:S(2)}, u32[]{:S(2)}) collective-permute-start(bf16[2,4,272,128]{3,2,1,0:T(8,128)(2,1)S(1)} %pad_maximum_fusion.4.own), channel_id=1, source_target_pairs={{0,2},{2,4},{4,6},{1,3},{3,5},{5,7},{8,10},{10,12},{12,14},{9,11},... | collective-permute-start | bytes 1671176 | tf_op jit(solution)/shard_map/ppermute | solution.py:178
  82.5 99.0 %collective-permute-start.16 = (bf16[2,4,272,128]{3,2,1,0:T(8,128)(2,1)S(1)}, bf16[2,4,272,128]{3,2,1,0:T(8,128)(2,1)}, u32[]{:S(2)}, u32[]{:S(2)}) collective-permute-start(bf16[2,4,272,128]{3,2,1,0:T(8,128)(2,1)S(1)} %pad_maximum_fusion.4.own), channel_id=1, source_target_pairs={{2,0},{4,2},{6,4},{3,1},{5,3},{7,5},{10,8},{12,10},{14,12},{11,9},... | collective-permute-start | bytes 1671176 | tf_op jit(solution)/shard_map/ppermute | solution.py:178
  83.8 97.7 %collective-permute-start.17 = (bf16[2,2,4,272,128]{4,3,2,1,0:T(8,128)(2,1)}, bf16[2,2,4,272,128]{4,3,2,1,0:T(8,128)(2,1)}, u32[]{:S(2)}, u32[]{:S(2)}) collective-permute-start(bf16[2,2,4,272,128]{4,3,2,1,0:T(8,128)(2,1)} %pad_maximum_fusion.1), channel_id=1, source_target_pairs={{0,2},{2,4},{4,6},{1,3},{3,5},{5,7},{8,10},{10,12},{12,14},{9,11},... | collective-permute-start | bytes 3342344 | tf_op jit(solution)/shard_map/ppermute | solution.py:178
  88.6 92.9 %collective-permute-start.18 = (bf16[2,2,4,272,128]{4,3,2,1,0:T(8,128)(2,1)}, bf16[2,2,4,272,128]{4,3,2,1,0:T(8,128)(2,1)}, u32[]{:S(2)}, u32[]{:S(2)}) collective-permute-start(bf16[2,2,4,272,128]{4,3,2,1,0:T(8,128)(2,1)} %pad_maximum_fusion.1), channel_id=1, source_target_pairs={{2,0},{4,2},{6,4},{3,1},{5,3},{7,5},{10,8},{12,10},{14,12},{11,9},... | collective-permute-start | bytes 3342344 | tf_op jit(solution)/shard_map/ppermute | solution.py:178
  89.9 1.1 copy-start.3
  90.9 1.1 copy-start.5
  92.0 1.0 copy-start.7
  92.9 1.0 copy-start.8
  123.0 0.7 copy-start.9
  123.8 0.7 copy-start.10
  126.6 8.2 %collective-permute-start.7 = (f32[4,2,272]{2,0,1:T(4,128)S(1)}, f32[4,2,272]{2,0,1:T(4,128)S(1)}, u32[]{:S(2)}, u32[]{:S(2)}) collective-permute-start(f32[4,2,272]{2,0,1:T(4,128)S(1)} %copy.109), channel_id=1, source_target_pairs={{0,8},{8,16},{16,24},{1,9},{9,17},{17,25},{2,10},{10,18},{18,26},{... | collective-permute-start | bytes 26120 | tf_op jit(solution)/shard_map/ppermute | solution.py:178
  134.8 5.6 %collective-permute-start.8 = (f32[4,2,272]{2,0,1:T(4,128)S(1)}, f32[4,2,272]{2,0,1:T(4,128)S(1)}, u32[]{:S(2)}, u32[]{:S(2)}) collective-permute-start(f32[4,2,272]{2,0,1:T(4,128)S(1)} %copy.109), channel_id=1, source_target_pairs={{8,0},{16,8},{24,16},{9,1},{17,9},{25,17},{10,2},{18,10},{26,18},{... | collective-permute-start | bytes 26120 | tf_op jit(solution)/shard_map/ppermute | solution.py:178
  140.5 3.1 %collective-permute-start.9 = (f32[4,2,272]{2,0,1:T(4,128)S(1)}, f32[4,2,272]{2,0,1:T(4,128)S(1)}, u32[]{:S(2)}, u32[]{:S(2)}) collective-permute-start(f32[4,2,272]{2,0,1:T(4,128)S(1)} %copy.109), channel_id=1, source_target_pairs={{0,2},{2,4},{4,6},{1,3},{3,5},{5,7},{8,10},{10,12},{12,14},{9,11},... | collective-permute-start | bytes 26120 | tf_op jit(solution)/shard_map/ppermute | solution.py:178
  143.6 5.5 %collective-permute-start.10 = (f32[4,2,272]{2,0,1:T(4,128)S(1)}, f32[4,2,272]{2,0,1:T(4,128)S(1)}, u32[]{:S(2)}, u32[]{:S(2)}) collective-permute-start(f32[4,2,272]{2,0,1:T(4,128)S(1)} %copy.109), channel_id=1, source_target_pairs={{2,0},{4,2},{6,4},{3,1},{5,3},{7,5},{10,8},{12,10},{14,12},{11,9},... | collective-permute-start | bytes 26120 | tf_op jit(solution)/shard_map/ppermute | solution.py:178
  149.1 5.7 %collective-permute-start.11 = (f32[2,4,2,272]{3,1,2,0:T(4,128)S(1)}, f32[2,4,2,272]{3,1,2,0:T(4,128)S(1)}, u32[]{:S(2)}, u32[]{:S(2)}) collective-permute-start(f32[2,4,2,272]{3,1,2,0:T(4,128)S(1)} %pad_maximum_fusion.8), channel_id=1, source_target_pairs={{0,2},{2,4},{4,6},{1,3},{3,5},{5,7},{8,10},{10,12},{12,14},{9,11},... | collective-permute-start | bytes 52232 | tf_op jit(solution)/shard_map/ppermute | solution.py:178
  154.8 3.1 %collective-permute-start.12 = (f32[2,4,2,272]{3,1,2,0:T(4,128)S(1)}, f32[2,4,2,272]{3,1,2,0:T(4,128)S(1)}, u32[]{:S(2)}, u32[]{:S(2)}) collective-permute-start(f32[2,4,2,272]{3,1,2,0:T(4,128)S(1)} %pad_maximum_fusion.8), channel_id=1, source_target_pairs={{2,0},{4,2},{6,4},{3,1},{5,3},{7,5},{10,8},{12,10},{14,12},{11,9},... | collective-permute-start | bytes 52232 | tf_op jit(solution)/shard_map/ppermute | solution.py:178
  157.9 12.9 %collective-permute-start.6 = (bf16[3,10,36,128]{3,2,1,0:T(8,128)(2,1)}, bf16[3,10,36,128]{3,2,1,0:T(8,128)(2,1)}, u32[]{:S(2)}, u32[]{:S(2)}) collective-permute-start(bf16[3,10,36,128]{3,2,1,0:T(8,128)(2,1)} %reshape.100), channel_id=1, source_target_pairs={{0,1},{1,0},{2,3},{3,2},{4,5},{5,4},{6,7},{7,6},{8,9},{9,8},{10,11... | collective-permute-start | bytes 829448 | tf_op jit(solution)/shard_map/ppermute | solution.py:284
  165.2 5.5 %copy-start.14 = (bf16[3,10,36,128]{3,2,1,0:T(8,128)(2,1)S(1)}, bf16[3,10,36,128]{3,2,1,0:T(8,128)(2,1)}, u32[]{:S(2)}) copy-start(bf16[3,10,36,128]{3,2,1,0:T(8,128)(2,1)} %reshape.100) | copy-start | bytes 829444
  171.8 0.7 copy-start.12
  171.8 0.8 copy-start.13
  172.6 4.5 %copy-start.17 = (f32[2]{0:T(128)S(1)}, f32[2]{0:T(128)}, u32[]{:S(2)}) copy-start(f32[2]{0:T(128)} %constant.30.clone) | copy-start | bytes 28
  177.1 4.4 %copy-start.1 = (f32[4,272,1]{2,1,0:T(8,128)S(1)}, f32[4,272,1]{2,1,0:T(8,128)}, u32[]{:S(2)}) copy-start(f32[4,272,1]{2,1,0:T(8,128)} %copy.122.live_ref) | copy-start | bytes 13060
  177.1 4.3 %copy-start.6 = (bf16[4,272,128]{2,1,0:T(8,128)(2,1)S(1)}, bf16[4,272,128]{2,1,0:T(8,128)(2,1)}, u32[]{:S(2)}) copy-start(bf16[4,272,128]{2,1,0:T(8,128)(2,1)} %get-tuple-element.49.k_ref) | copy-start | bytes 835588
  202.3 0.7 copy-start.11
Sparse Core Ops, SparseCore 0:
  20.1 17.9 reduce-scatter.6
  177.2 59.5 reduce-scatter.4

commit v2 on v1

--- a/solution.py
+++ b/solution.py
@@ -23,45 +23,125 @@
     )
 
 
-def gather_tiles(pieces, dests, sems, block):
-    copies = []
-    index = 0
-    for piece in pieces:
-        for which, dest in enumerate(dests):
-            copies.append((piece.at[which], dest))
-    started = []
-    for index, (source, dest) in enumerate(copies):
-        slot = index // len(dests)
-        copy = pltpu.make_async_copy(
-            source, dest.at[:, slot * block : (slot + 1) * block, :], sems.at[index]
-        )
-        copy.start()
-        started.append(copy)
-    return started
-
-
-def split_pieces(own, near, far):
-    views = [own]
-    views += list(near)
-    for pair in far:
-        views += [pair.at[0], pair.at[1]]
-    return views
+MESH = pl.DeviceIdType.MESH
 
 
 def query_kernel(
-    q_ref, g_ref, bias_ref, own, t_prev, t_next, w_prev, w_next, c_prev, c_next,
-    att_ref, gq_ref, stats_ref,
-    k_all, v_all, s_buf, top, tot, out, grad, sems,
+    k_ref, v_ref, q_ref, part_own, part_other, bias_ref,
+    att_ref, other_ref, gq_ref, q_all, g_all, stats_ref,
+    k_all, v_all, s_buf, top, tot, out, grad, part_in, att_in, st_own, st_all,
+    send_sem, recv_sem, own_sem, peer_send, peer_recv,
     *, tiles, block, wide, chunk, scale,
 ):
     per = wide // chunk
     depth = q_ref.shape[-1]
+    t_index, w_index, h_index = (lax.axis_index(name) for name in ("tm", "width", "head"))
+    t_back, t_ahead = t_index > 0, t_index < lax.axis_size("tm") - 1
+    w_back, w_ahead = w_index > 0, w_index < lax.axis_size("width") - 1
+    exists = [
+        None, t_back, t_ahead, w_back, w_ahead,
+        t_back & w_back, t_ahead & w_back, t_back & w_ahead, t_ahead & w_ahead,
+    ]
+    t_above = (t_index + 1, w_index, h_index)
+    t_below = (t_index - 1, w_index, h_index)
+    w_above = (t_index, w_index + 1, h_index)
+    w_below = (t_index, w_index - 1, h_index)
+    peer = (t_index, w_index, 1 - h_index)
+    direct = [(1, t_ahead, t_above), (2, t_back, t_below), (3, w_ahead, w_above), (4, w_back, w_below)]
+    onward = [
+        (5, 1, t_back & w_ahead, w_above), (7, 1, t_back & w_back, w_below),
+        (6, 2, t_ahead & w_ahead, w_above), (8, 2, t_ahead & w_back, w_below),
+    ]
+
+    def slot_of(which, slot):
+        if which == 4:
+            return st_all.at[slot]
+        dest = (k_all, v_all, q_all, g_all)[which]
+        return dest.at[:, slot * block : (slot + 1) * block, :]
+
+    def remote(which, source, slot, device):
+        return pltpu.make_async_remote_copy(
+            src_ref=source, dst_ref=slot_of(which, slot),
+            send_sem=send_sem.at[which, slot], recv_sem=recv_sem.at[which, slot],
+            device_id=device, device_id_type=MESH,
+        )
+
+    def send_direct(which, source):
+        for slot, there, device in direct:
+            @pl.when(there)
+            def _():
+                remote(which, source, slot, device).start()
+
+    def send_onward(which):
+        for slot, via, there, device in onward:
+            @pl.when(there)
+            def _():
+                remote(which, slot_of(which, via), slot, device).start()
+
+    def receive(which, slots):
+        for slot in slots:
+            @pl.when(exists[slot])
+            def _():
+                remote(which, slot_of(which, slot), slot, peer).wait_recv()
+
+    def sent(which, source):
+        for slot, there, device in direct:
+            @pl.when(there)
+            def _():
+                remote(which, source, slot, device).wait_send()
+        for slot, via, there, device in onward:
+            @pl.when(there)
+            def _():
+                remote(which, slot_of(which, via), slot, device).wait_send()
+
+    barrier = pltpu.get_barrier_semaphore()
+    for _, there, device in direct:
+        @pl.when(there)
+        def _():
+            pl.semaphore_signal(barrier, inc=1, device_id=device, device_id_type=MESH)
+    pl.semaphore_signal(barrier, inc=1, device_id=peer, device_id_type=MESH)
+    greeted = 1 + sum(jnp.where(there, 1, 0) for _, there, _ in direct)
+    pl.semaphore_wait(barrier, greeted)
+
+    def swap_part():
+        return pltpu.make_async_remote_copy(
+            src_ref=part_other, dst_ref=part_in, send_sem=peer_send.at[0],
+            recv_sem=peer_recv.at[0], device_id=peer, device_id_type=MESH,
+        )
+
+    def swap_att():
+        return pltpu.make_async_remote_copy(
+            src_ref=att_ref, dst_ref=att_in, send_sem=peer_send.at[1],
+            recv_sem=peer_recv.at[1], device_id=peer, device_id_type=MESH,
+        )
+
+    swap_part().start()
+    send_direct(0, k_ref)
+    send_direct(1, v_ref)
+    for which, source in enumerate((k_ref, v_ref, q_ref)):
+        pltpu.make_async_copy(source, slot_of(which, 0), own_sem.at[which]).start()
     fill = jnp.zeros((tiles, wide - 9 * block, depth), jnp.bfloat16)
-    k_all[:, 9 * block :, :] = fill
-    v_all[:, 9 * block :, :] = fill
-    pieces = split_pieces(own, (t_prev, t_next, w_prev, w_next), (c_prev, c_next))
-    for copy in gather_tiles(pieces, (k_all, v_all), sems, block):
-        copy.wait()
+    hole = jnp.zeros((tiles, block, depth), jnp.bfloat16)
+    for dest in (k_all, v_all, q_all, g_all):
+        dest[:, 9 * block :, :] = fill
+        for slot in range(1, 9):
+            @pl.when(jnp.logical_not(exists[slot]))
+            def _():
+                dest[:, slot * block : (slot + 1) * block, :] = hole
+    swap_part().wait()
+    g_all[:, :block, :] = (
+        part_own[...].astype(jnp.float32) + part_in[...].astype(jnp.float32)
+    ).astype(jnp.bfloat16)
+    for which, source in enumerate((k_ref, v_ref, q_ref)):
+        pltpu.make_async_copy(source, slot_of(which, 0), own_sem.at[which]).wait()
+    receive(0, (1, 2))
+    send_onward(0)
+    receive(1, (1, 2))
+    send_onward(1)
+    send_direct(2, q_ref)
+    send_direct(3, slot_of(3, 0))
+    receive(0, (3, 4, 5, 6, 7, 8))
+    receive(1, (3, 4, 5, 6, 7, 8))
 
     @pl.loop(0, tiles)
     def _(tile):
@@ -71,6 +151,12 @@
         tot[...] = jnp.zeros(tot.shape, jnp.float32)
         out[...] = jnp.zeros(out.shape, jnp.float32)
         grad[...] = jnp.zeros(grad.shape, jnp.float32)
+
+        @pl.when(tile == tiles // 2)
+        def _():
+            for which in (2, 3):
+                receive(which, (1, 2))
+                send_onward(which)
 
         @pl.loop(low, high)
         def _(step):
@@ -103,20 +189,24 @@
                 preferred_element_type=jnp.float32,
             )
 
+        grads = g_all[tile, :block, :]
         total = jnp.sum(tot[...], axis=1, keepdims=True)
         attended = (out[...] / total).astype(jnp.bfloat16)
         att_ref[tile] = attended
         delta = jnp.sum(
-            g_ref[tile].astype(jnp.float32) * attended.astype(jnp.float32), axis=1, keepdims=True
+            grads.astype(jnp.float32) * attended.astype(jnp.float32), axis=1, keepdims=True
         )
         lanes = lax.broadcasted_iota(jnp.int32, (block, 128), 1)
-        stats_ref[tile] = jnp.where(lanes == 0, peak + jnp.log2(total), delta)
+        columns = jnp.where(lanes == 0, peak + jnp.log2(total), delta)
+        span = st_own.shape[-1]
+        columns = jnp.concatenate([columns, jnp.zeros((span - block, 128), jnp.float32)], axis=0)
+        st_own[tile] = columns.T[:8]
 
         @pl.loop(low, high)
         def _(step):
             row = step // per
             start = pl.multiple_of((step % per) * chunk, chunk)
-            dprob = dot_nt(g_ref[tile], v_all[row, pl.ds(start, chunk), :])
+            dprob = dot_nt(grads, v_all[row, pl.ds(start, chunk), :])
             dscore = (s_buf[step - low] * (dprob - delta)).astype(jnp.bfloat16)
             grad[...] += jnp.dot(
                 dscore, k_all[row, pl.ds(start, chunk), :], preferred_element_type=jnp.float32
@@ -124,21 +214,30 @@
 
         gq_ref[tile] = (grad[...] * (scale / total)).astype(jnp.bfloat16)
 
+    swap_att().start()
+    send_direct(4, st_own)
+    first = lax.broadcasted_iota(jnp.int32, (tiles, 8, wide), 1) == 0
+    stats_ref[...] = jnp.where(first, FAR, 0.0)
+    stats_ref[:, :, :block] = st_own[:, :, :block]
+    receive(4, (1, 2))
+    send_onward(4)
+    for which in (2, 3, 4):
+        receive(which, (3, 4, 5, 6, 7, 8))
+    for slot in range(1, 9):
+        @pl.when(exists[slot])
+        def _():
+            stats_ref[:, :, slot * block : (slot + 1) * block] = st_all[slot, :, :, :block]
+    for which, source in enumerate((k_ref, v_ref, q_ref, slot_of(3, 0), st_own)):
+        sent(which, source)
+    swap_att().wait()
+    other_ref[...] = att_in[...]
+
 
 def key_kernel(
-    k_ref, v_ref, live_ref, stats_ref, own, t_prev, t_next, w_prev, w_next, c_prev, c_next,
-    gk_ref, gv_ref,
-    q_all, g_all, grad_k, grad_v, sems,
+    k_ref, v_ref, live_ref, stats_ref, q_all, g_all, gk_ref, gv_ref, grad_k, grad_v,
     *, tiles, block, wide, chunk, scale,
 ):
     per = wide // chunk
-    depth = k_ref.shape[-1]
-    fill = jnp.zeros((tiles, wide - 9 * block, depth), jnp.bfloat16)
-    q_all[:, 9 * block :, :] = fill
-    g_all[:, 9 * block :, :] = fill
-    pieces = split_pieces(own, (t_prev, t_next, w_prev, w_next), (c_prev, c_next))
-    for copy in gather_tiles(pieces, (q_all, g_all), sems, block):
-        copy.wait()
 
     @pl.loop(0, tiles)
     def _(tile):
@@ -169,27 +268,6 @@
         gv_ref[tile] = jnp.where(live, grad_v[...], 0.0).astype(jnp.bfloat16)
 
 
-def shift(cells, axis, forward):
-    count = lax.axis_size(axis)
-    if forward:
-        pairs = [(i, i + 1) for i in range(count - 1)]
-    else:
-        pairs = [(i + 1, i) for i in range(count - 1)]
-    return lax.ppermute(cells, axis, pairs)
-
-
-def neighbours(cells):
-    t_prev = shift(cells, "tm", True)
-    t_next = shift(cells, "tm", False)
-    w_prev = shift(cells, "width", True)
-    w_next = shift(cells, "width", False)
-    pair = jnp.stack([t_prev, t_next])
-    return (
-        cells, t_prev, t_next, w_prev, w_next,
-        shift(pair, "width", True), shift(pair, "width", False),
-    )
-
-
 def lay_out(cells, block, tile_rows):
     frames, columns, rows, depth = cells.shape
     tiles = rows // tile_rows
@@ -234,20 +312,18 @@
     wide_live = jnp.pad(wide_live, ((0, 0), (0, wide - 9 * block)))
     bias = jnp.where(wide_live, 0.0, -FAR).astype(jnp.float32)[:, None, :]
 
-    key_value = neighbours(jnp.stack([key, value]))
     grad_heads = lax.dot_general(
         grad_in, out_weight, (((3,), (1,)), ((), ())), preferred_element_type=jnp.float32
     )
-    grad_own = lax.psum_scatter(
-        grad_heads.astype(jnp.bfloat16), "head", scatter_dimension=3, tiled=True
-    )
-    grad_own = lay_out(grad_own, block, TH)
-    query_grad = neighbours(jnp.stack([query, grad_own]))
+    parts = lay_out(grad_heads.astype(jnp.bfloat16), block, TH)
+    low_part, high_part = parts[..., :depth], parts[..., depth:]
+    first = lax.axis_index("head") == 0
+    part_own = jnp.where(first, low_part, high_part)
+    part_other = jnp.where(first, high_part, low_part)
 
     pairs = tiles * 3 - 2
     work = pairs * block * wide
     in_vmem = pl.BlockSpec(memory_space=pltpu.VMEM)
-    in_any = pl.BlockSpec(memory_space=pl.ANY)
     params = dict(tiles=tiles, block=block, wide=wide, chunk=chunk, scale=scale)
     flat = jax.ShapeDtypeStruct((tiles, block, depth), jnp.bfloat16)
     wide_bf16 = pltpu.VMEM((tiles, wide, depth), jnp.bfloat16)
@@ -256,33 +332,38 @@
     cost = pl.CostEstimate(
         flops=16 * work * depth, transcendentals=work, bytes_accessed=4 * tiles * wide * depth
     )
-    attended, grad_query, stats = pl.pallas_call(
+    spread = jax.ShapeDtypeStruct((tiles, wide, depth), jnp.bfloat16)
+    span = round_up(block, 128)
+    tile_bf16 = pltpu.VMEM((tiles, block, depth), jnp.bfloat16)
+    attended, other, grad_query, query_wide, grad_wide, stats_wide = pl.pallas_call(
         functools.partial(query_kernel, **params),
-        out_shape=(flat, flat, jax.ShapeDtypeStruct((tiles, block, 128), jnp.float32)),
-        in_specs=[in_vmem] * 3 + [in_any] * 7,
-        out_specs=(in_vmem, in_vmem, in_vmem),
+        out_shape=(
+            flat, flat, flat, spread, spread,
+            jax.ShapeDtypeStruct((tiles, 8, wide), jnp.float32),
+        ),
+        in_specs=[in_vmem] * 6,
+        out_specs=(in_vmem,) * 6,
         scratch_shapes=[
             wide_bf16, wide_bf16,
             pltpu.VMEM((min(3, tiles) * (wide // chunk), block, chunk), jnp.float32),
-            lane_acc, lane_acc, acc, acc,
-            pltpu.SemaphoreType.DMA((18,)),
+            lane_acc, lane_acc, acc, acc, tile_bf16, tile_bf16,
+            pltpu.VMEM((tiles, 8, span), jnp.float32),
+            pltpu.VMEM((9, tiles, 8, span), jnp.float32),
+            pltpu.SemaphoreType.DMA((5, 9)),
+            pltpu.SemaphoreType.DMA((5, 9)),
+            pltpu.SemaphoreType.DMA((3,)),
+            pltpu.SemaphoreType.DMA((2,)),
+            pltpu.SemaphoreType.DMA((2,)),
         ],
-        compiler_params=pltpu.CompilerParams(vmem_limit_bytes=50 << 20),
+        compiler_params=pltpu.CompilerParams(
+            vmem_limit_bytes=56 << 20, collective_id=0, has_side_effects=True
+        ),
         cost_estimate=cost,
         name="query_side",
-    )(query, grad_own, bias, *key_value)
-
-    stats_own = stats[:, :, :2].transpose(0, 2, 1)
-    near = neighbours(stats_own)
-    joined = jnp.stack(list(near[:5]) + [near[5][0], near[5][1], near[6][0], near[6][1]], axis=2)
-    blank = jnp.array([FAR, 0.0], jnp.float32)[None, :, None, None]
-    joined = jnp.where(exists[None, None, :, None], joined, blank).reshape(tiles, 2, 9 * block)
-    tail = jnp.broadcast_to(blank[..., 0], (tiles, 2, wide - 9 * block))
-    stats_wide = jnp.concatenate([joined, tail], axis=2)
+    )(key, value, query, part_own, part_other, bias)
 
     attended = lay_back(attended, frames, columns, TH)
-    other = lax.ppermute(attended, "head", [(0, 1), (1, 0)])
-    first = lax.axis_index("head") == 0
+    other = lay_back(other, frames, columns, TH)
     heads_all = jnp.concatenate(
         [jnp.where(first, attended, other), jnp.where(first, other, attended)], axis=3
     )
@@ -301,13 +382,13 @@
     grad_key, grad_value = pl.pallas_call(
         functools.partial(key_kernel, **params),
         out_shape=(flat, flat),
-        in_specs=[in_vmem] * 4 + [in_any] * 7,
+        in_specs=[in_vmem] * 6,
         out_specs=(in_vmem, in_vmem),
-        scratch_shapes=[wide_bf16, wide_bf16, acc, acc, pltpu.SemaphoreType.DMA((18,))],
+        scratch_shapes=[acc, acc],
         compiler_params=pltpu.CompilerParams(vmem_limit_bytes=50 << 20),
         cost_estimate=cost,
         name="key_side",
-    )(key, value, live_rows, stats_wide, *query_grad)
+    )(key, value, live_rows, stats_wide, query_wide, grad_wide)
 
     back = lambda cells: lay_back(cells, frames, columns, TH).transpose(swap)
     return (mixed.transpose(swap), back(grad_query), back(grad_key), back(grad_value), grad_weight)

time: 245 us -> 155 us (0.63)
  local copies, waits for them, and re-layouts: 55.8 us -> 9.31 us
  starting transfers between devices: 45.4 us -> 0.04 us
  Pallas kernels: 49.9 us -> 83.9 us
  waiting for transfers between devices: 61.1 us -> 33.5 us
    ppermute x19 -> x0, starting transfers between devices: 45.3 us -> none  [the longest x18 44.8 us: shift(): return lax.ppermute(cells, axis, pairs)]
    pallas_call x1, Pallas kernels: 29.2 us -> 62.9 us  [shards(): pl.pallas_call(functools.partial(query_kernel, **params), out_shape=(flat...]
    unnamed x57 -> x20, local copies, waits for them, and re-layouts: 36.1 us -> 2.81 us
    ppermute x19 -> x0, waiting for transfers between devices: 21.3 us -> none  [the longest x18 21.3 us: shift(): return lax.ppermute(cells, axis, pairs)]
    unnamed x3 -> x1, waiting for transfers between devices: 9.1 us -> 0.02 us
    another operation x4 -> x0, local copies, waits for them, and re-layouts: 7.33 us -> none  [the longest x3 6.38 us: shards(): jnp.stack(list(near[:5]) + [near[5][0], near[5][1], near[6][0], near[6][1...]
    another operation x5 -> x0, other arithmetic: 3.66 us -> none  [the longest x3 3.55 us: neighbours(): pair = jnp.stack([t_prev, t_next])]
    slice x4 -> x3, local copies, waits for them, and re-layouts: 3.36 us -> 0.32 us  [lay_back(): cells = cells[:, :count * tile_rows].reshape(tiles, count, tile_rows, depth)]
  transfers between devices with their start and end apart: 21 -> 1, of which waited for: 6 -> 1; matrix products, arithmetic and copies ran while one was open for 22% -> 4% of each run, Pallas kernels for 21% -> 14%
where the time goes in v2:
time: 155 us
  Pallas kernels  83.9 us (54%)
  waiting for transfers between devices  33.5 us (22%)
  between operations  14.4 us (9%)
  matrix products  10.7 us (7%)
  local copies, waits for them, and re-layouts  9.31 us (6%)
  other arithmetic  2.73 us (2%)
    pallas_call x1, Pallas kernels, shards(): pl.pallas_call(functools.partial(query_kernel, **params), out_shape=(flat...  62.9 us
    reduce_scatter x1, waiting for transfers between devices, shards(): lax.psum_scatter(lax.dot_general(heads_all, grad_in, (((0, 1, 2), (0, 1,...  33.5 us
    pallas_call x1, Pallas kernels, shards(): pl.pallas_call(functools.partial(key_kernel, **params), out_shape=(flat,...  21 us
    dot_general x1, matrix products, shards(): lax.dot_general(heads_all, grad_in, (((0, 1, 2), (0, 1, 2)), ((), ())), p...  4.52 us
    dot_general x1, matrix products, shards(): lax.dot_general(grad_in, out_weight, (((3,), (1,)), ((), ())), preferred_...  3.25 us
  transfers between devices with their start and end apart: 1, of which 1 were waited for; matrix products, arithmetic and copies ran while one was open for 4% of the time, Pallas kernels for 14%

profile of v2, /device:TPU:0, one launch (start us, length us, event | category | flops | bytes accessed | tf_op | source)
XLA Modules:
  0.0 154.6 jit_solution(17738152160107271065)
XLA Ops:
  7.2 0.0 reduce-scatter.2.cloned.1.call-start
  7.2 0.1 stack.39
  7.4 0.1 and.41
  7.4 0.1 and.42
  7.5 0.7 broadcast_compare_fusion
  8.2 0.1 broadcast_in_dim.25
  8.3 0.1 reshape.82
  8.5 0.1 and.36
  8.6 0.6 broadcast_in_dim.29.bias_ref
  9.3 3.3 %fusion.8 = bf16[3,10,36,256]{3,2,1,0:T(8,128)(2,1)S(1)} fusion(bf16[3,36,10,1536]{3,1,2,0:T(8,128)(2,1)} %param.11, bf16[256,1536]{1,0:T(8,128)(2,1)S(1)} %copy-done), kind=kOutput, calls=%fused_computation.7 | convolution fusion | flops 849623040 | bytes 4657152 | tf_op jit(solution)/shard_map/dot_general | solution.py:315
  12.6 0.2 reshape.95
  12.8 0.3 copy.30
  13.1 0.1 copy.31
  13.2 0.3 copy-done.4
  13.5 0.1 reshape.92
  13.6 0.1 copy.21
  13.8 0.1 reshape.93
  13.9 0.1 copy.24
  14.1 0.7 pad.22.k_ref
  14.8 0.7 pad.23.v_ref
  15.5 0.1 reshape.94
  15.6 0.1 copy.27
  15.8 0.7 pad.24.q_ref
  16.5 0.9 broadcast_select_fusion
  17.5 62.9 %query_side.1 = (bf16[4,272,128]{2,1,0:T(8,128)(2,1)}, bf16[4,272,128]{2,1,0:T(8,128)(2,1)}, bf16[4,272,128]{2,1,0:T(8,128)(2,1)}, bf16[4,2560,128]{2,1,0:T(8,12...) custom-call(bf16[4,272,128]{2,1,0:T(8,128)(2,1)} %pad.22.k_ref, bf16[4,272,128]{2,1,0:T(8,128)(2,1)} %pad.23.v_ref, ...), custom_call_target="tpu_custom_call" | custom-call | flops 14260633600 | bytes 5242880 | tf_op jit(solution)/shard_map/query_side/pallas_call | solution.py:338
  80.4 1.1 broadcast_select_fusion.2
  81.5 0.1 copy.32
  81.6 0.1 copy.58
  81.7 0.1 reshape.96
  81.8 0.1 constant_dynamic-update-slice_fusion.1
  81.9 0.1 copy.34
  82.0 0.1 copy.59
  82.1 0.1 reshape.97
  82.2 0.1 constant_dynamic-update-slice_fusion
  82.4 4.5 %fusion.5 = f32[256,1536]{1,0:T(8,128)} fusion(bf16[3,10,36,256]{3,2,1,0:T(8,128)(2,1)S(1)} %constant_dynamic-update-slice_fusion, bf16[3,36,10,1536]{3,1,2,0:T(8,128)(2,1)} %param.11), kind=kOutput, calls=%fused_computation.6 | convolution fusion | flops 849346560 | bytes 5443584 | tf_op jit(solution)/shard_map/dot_general | solution.py:374
  86.9 0.2 copy.40.live_ref
  87.2 21.0 %key_side.1 = (bf16[4,272,128]{2,1,0:T(8,128)(2,1)S(1)}, bf16[4,272,128]{2,1,0:T(8,128)(2,1)S(1)}) custom-call(bf16[4,272,128]{2,1,0:T(8,128)(2,1)S(1)} %copy-done.1, bf16[4,272,128]{2,1,0:T(8,128)(2,1)S(1)} %copy-done.2, f32[4,272,1]{2,1,0:T(8,128)S(1)} %copy.40.live_ref, f32[4,8,2560]{2,1,0:T(8,128)S(1)} %copy-done.3, ...), custom_call_target="tpu_custom_call" | custom-call | flops 14260633600 | bytes 5242880 | tf_op jit(solution)/shard_map/key_side/pallas_call | solution.py:382
  108.2 0.1 copy.41
  108.3 0.1 reshape.86
  108.4 0.8 copy.46
  109.2 0.1 copy.43
  109.4 0.1 reshape.88
  109.5 0.8 copy.47
  110.3 0.1 copy.38
  110.5 0.1 reshape.84
  110.5 0.8 copy.45
  111.3 3.0 %fusion.4 = bf16[3,36,10,1536]{3,1,2,0:T(8,128)(2,1)} fusion(bf16[3,10,36,256]{3,2,1,0:T(8,128)(2,1)S(1)} %constant_dynamic-update-slice_fusion, bf16[256,1536]{1,0:T(8,128)(2,1)S(1)} %copy-done), kind=kOutput, calls=%fused_computation.5 | convolution fusion | flops 851005440 | bytes 4657152 | tf_op jit(solution)/shard_map/dot_general | solution.py:370
  114.3 33.5 %reduce-scatter.2.cloned.1.call-done = f32[16,1536]{1,0:T(8,128)} async-done(((f32[256,1536]{1,0:T(8,128)}), f32[16,1536]{1,0:T(8,128)}) %reduce-scatter.2.cloned.1.call-update) | async-done | bytes 98320 | tf_op jit(solution)/shard_map/reduce_scatter | solution.py:373
  (27 shorter events, 0.4 us)
Async XLA Ops:
  7.2 2.1 %copy-start = (bf16[256,1536]{1,0:T(8,128)(2,1)S(1)}, bf16[256,1536]{1,0:T(8,128)(2,1)}, u32[]{:S(2)}) copy-start(bf16[256,1536]{1,0:T(8,128)(2,1)} %param.10) | copy-start | bytes 2359300
  7.2 140.6 %reduce-scatter.2.cloned.1.call-start = ((), (), s32[]{:S(2)}) async-start(), calls=%async_computation.1 | async-start | bytes 1671168 | tf_op jit(solution)/shard_map/reduce_scatter | solution.py:373
  12.5 1.0 copy-start.4
  12.5 1.2 copy-start.5
  12.8 2.8 %copy-start.6 = (bf16[3,36,10,128]{3,1,2,0:T(8,128)(2,1)S(1)}, bf16[3,36,10,128]{3,1,2,0:T(8,128)(2,1)}, u32[]{:S(2)}) copy-start(bf16[3,36,10,128]{3,1,2,0:T(8,128)(2,1)} %param.6) | copy-start | bytes 829444
  82.3 4.8 %copy-start.1 = (bf16[4,272,128]{2,1,0:T(8,128)(2,1)S(1)}, bf16[4,272,128]{2,1,0:T(8,128)(2,1)}, u32[]{:S(2)}) copy-start(bf16[4,272,128]{2,1,0:T(8,128)(2,1)} %pad.22.k_ref) | copy-start | bytes 835588
  82.3 4.8 %copy-start.2 = (bf16[4,272,128]{2,1,0:T(8,128)(2,1)S(1)}, bf16[4,272,128]{2,1,0:T(8,128)(2,1)}, u32[]{:S(2)}) copy-start(bf16[4,272,128]{2,1,0:T(8,128)(2,1)} %pad.23.v_ref) | copy-start | bytes 835588
  82.4 4.8 %copy-start.3 = (f32[4,8,2560]{2,1,0:T(8,128)S(1)}, f32[4,8,2560]{2,1,0:T(8,128)}, u32[]{:S(2)}) copy-start(f32[4,8,2560]{2,1,0:T(8,128)} %get-tuple-element.16.stats_ref) | copy-start | bytes 983044
  108.2 2.1 %copy-start.7 = (bf16[4,272,128]{2,1,0:T(8,128)(2,1)S(1)}, bf16[4,272,128]{2,1,0:T(8,128)(2,1)}, u32[]{:S(2)}) copy-start(bf16[4,272,128]{2,1,0:T(8,128)(2,1)} %get-tuple-element.15) | copy-start | bytes 835588
Sparse Core Ops, SparseCore 0:
  87.0 60.7 reduce-scatter.1

commit v3 on v2

--- a/solution.py
+++ b/solution.py
@@ -234,15 +234,61 @@
 
 
 def key_kernel(
-    k_ref, v_ref, live_ref, stats_ref, q_all, g_all, gk_ref, gv_ref, grad_k, grad_v,
+    k_ref, v_ref, live_ref, stats_ref, q_all, g_all, gw_ref,
+    gk_ref, gv_ref, share_ref,
+    grad_k, grad_v, in_w, in_t, sum_w, send_t, w_send, w_recv, t_send, t_recv,
     *, tiles, block, wide, chunk, scale,
 ):
     per = wide // chunk
+    t_index, w_index, h_index = (lax.axis_index(name) for name in ("tm", "width", "head"))
+    t_count, w_count = lax.axis_size("tm"), lax.axis_size("width")
+
+    def w_copy(hop):
+        dest = lax.rem(w_index + hop, w_count)
+        return pltpu.make_async_remote_copy(
+            src_ref=gw_ref.at[:, dest], dst_ref=in_w.at[hop - 1],
+            send_sem=w_send.at[hop - 1], recv_sem=w_recv.at[hop - 1],
+            device_id=(t_index, dest, h_index), device_id_type=MESH,
+        )
+
+    def t_copy(hop):
+        dest = lax.rem(t_index + hop, t_count)
+        return pltpu.make_async_remote_copy(
+            src_ref=send_t.at[dest], dst_ref=in_t.at[hop - 1],
+            send_sem=t_send.at[hop - 1], recv_sem=t_recv.at[hop - 1],
+            device_id=(dest, w_index, h_index), device_id_type=MESH,
+        )
+
+    barrier = pltpu.get_barrier_semaphore()
+    for hop in range(1, w_count):
+        pl.semaphore_signal(
+            barrier, inc=1, device_id=(t_index, lax.rem(w_index + hop, w_count), h_index),
+            device_id_type=MESH,
+        )
+    for hop in range(1, t_count):
+        pl.semaphore_signal(
+            barrier, inc=1, device_id=(lax.rem(t_index + hop, t_count), w_index, h_index),
+            device_id_type=MESH,
+        )
+    pl.semaphore_wait(barrier, w_count + t_count - 2)
+    for hop in range(1, w_count):
+        w_copy(hop).start()
 
     @pl.loop(0, tiles)
     def _(tile):
         low = jnp.maximum(tile - 1, 0) * per
         high = (jnp.minimum(tile + 1, tiles - 1) + 1) * per
+        @pl.when(tile == tiles // 2)
+        def _():
+            whole = gw_ref[:, w_index].astype(jnp.float32)
+            for hop in range(1, w_count):
+                w_copy(hop).wait()
+                whole = whole + in_w[hop - 1].astype(jnp.float32)
+            sum_w[...] = whole
+            send_t[...] = whole.astype(jnp.bfloat16)
+            for hop in range(1, t_count):
+                t_copy(hop).start()
+
         grad_k[...] = jnp.zeros(grad_k.shape, jnp.float32)
         grad_v[...] = jnp.zeros(grad_v.shape, jnp.float32)
 
@@ -266,6 +312,12 @@
         live = live_ref[tile] > 0
         gk_ref[tile] = jnp.where(live, grad_k[...] * scale, 0.0).astype(jnp.bfloat16)
         gv_ref[tile] = jnp.where(live, grad_v[...], 0.0).astype(jnp.bfloat16)
+
+    share = sum_w[t_index]
+    for hop in range(1, t_count):
+        t_copy(hop).wait()
+        share = share + in_t[hop - 1].astype(jnp.float32)
+    share_ref[...] = share
 
 
 def lay_out(cells, block, tile_rows):
@@ -370,25 +422,36 @@
     mixed = lax.dot_general(
         heads_all, out_weight, (((3,), (0,)), ((), ())), preferred_element_type=jnp.float32
     ).astype(jnp.bfloat16)
-    grad_weight = lax.psum_scatter(
-        lax.dot_general(
-            heads_all, grad_in, (((0, 1, 2), (0, 1, 2)), ((), ())),
-            preferred_element_type=jnp.float32,
+    t_count, w_count = lax.axis_size("tm"), lax.axis_size("width")
+    share_rows, width = out_weight.shape[0] // (t_count * w_count), out_weight.shape[1]
+    terms = lax.dot_general(
+        heads_all, grad_in, (((0, 1, 2), (0, 1, 2)), ((), ())),
+        preferred_element_type=jnp.float32,
+    ).astype(jnp.bfloat16).reshape(t_count, w_count, share_rows, width)
+
+    live_rows = live.astype(jnp.float32)[:, :, None]
+    grad_key, grad_value, grad_weight = pl.pallas_call(
+        functools.partial(key_kernel, **params),
+        out_shape=(flat, flat, jax.ShapeDtypeStruct((share_rows, width), jnp.float32)),
+        in_specs=[in_vmem] * 7,
+        out_specs=(in_vmem,) * 3,
+        scratch_shapes=[
+            acc, acc,
+            pltpu.VMEM((w_count - 1, t_count, share_rows, width), jnp.bfloat16),
+            pltpu.VMEM((t_count - 1, share_rows, width), jnp.bfloat16),
+            pltpu.VMEM((t_count, share_rows, width), jnp.float32),
+            pltpu.VMEM((t_count, share_rows, width), jnp.bfloat16),
+            pltpu.SemaphoreType.DMA((w_count - 1,)),
+            pltpu.SemaphoreType.DMA((w_count - 1,)),
+            pltpu.SemaphoreType.DMA((t_count - 1,)),
+            pltpu.SemaphoreType.DMA((t_count - 1,)),
+        ],
+        compiler_params=pltpu.CompilerParams(
+            vmem_limit_bytes=50 << 20, collective_id=1, has_side_effects=True
         ),
-        ("tm", "width"), scatter_dimension=0, tiled=True,
-    )
-
-    live_rows = live.astype(jnp.float32)[:, :, None]
-    grad_key, grad_value = pl.pallas_call(
-        functools.partial(key_kernel, **params),
-        out_shape=(flat, flat),
-        in_specs=[in_vmem] * 6,
-        out_specs=(in_vmem, in_vmem),
-        scratch_shapes=[acc, acc],
-        compiler_params=pltpu.CompilerParams(vmem_limit_bytes=50 << 20),
         cost_estimate=cost,
         name="key_side",
-    )(key, value, live_rows, stats_wide, query_wide, grad_wide)
+    )(key, value, live_rows, stats_wide, query_wide, grad_wide, terms)
 
     back = lambda cells: lay_back(cells, frames, columns, TH).transpose(swap)
     return (mixed.transpose(swap), back(grad_query), back(grad_key), back(grad_value), grad_weight)

time: 155 us -> 113 us (0.73)
  waiting for transfers between devices: 33.5 us -> 0 us
  between operations: 14.4 us -> 1.02 us
  Pallas kernels: 83.9 us -> 87.1 us
  local copies, waits for them, and re-layouts: 9.31 us -> 11.1 us
    reduce_scatter x1 -> x0, waiting for transfers between devices: 33.5 us -> none  [shards(): lax.psum_scatter(lax.dot_general(heads_all, grad_in, (((0, 1, 2), (0, 1,...]
    pallas_call x1, Pallas kernels: 21 us -> 24.2 us  [shards(): pl.pallas_call(functools.partial(key_kernel, **params), out_shape=(flat,...]
    unnamed x20 -> x21, local copies, waits for them, and re-layouts: 2.81 us -> 3.84 us
  transfers between devices with their start and end apart: 1 -> 0, of which waited for: 1 -> 0; matrix products, arithmetic and copies ran while one was open for 4% -> 0% of each run, Pallas kernels for 14% -> 0%
where the time goes in v3:
time: 113 us
  Pallas kernels  87.1 us (77%)
  local copies, waits for them, and re-layouts  11.1 us (10%)
  matrix products  10.7 us (9%)
  other arithmetic  2.72 us (2%)
    pallas_call x1, Pallas kernels, shards(): pl.pallas_call(functools.partial(query_kernel, **params), out_shape=(flat...  62.9 us
    pallas_call x1, Pallas kernels, shards(): pl.pallas_call(functools.partial(key_kernel, **params), out_shape=(flat,...  24.2 us
    dot_general x1, matrix products, shards(): lax.dot_general(heads_all, out_weight, (((3,), (0,)), ((), ())), preferre...  4.05 us
    unnamed x21, local copies, waits for them, and re-layouts  3.84 us
    dot_general x1, matrix products, shards(): lax.dot_general(heads_all, grad_in, (((0, 1, 2), (0, 1, 2)), ((), ())), p...  3.44 us
    dot_general x1, matrix products, shards(): lax.dot_general(grad_in, out_weight, (((3,), (1,)), ((), ())), preferred_...  3.26 us

profile of v3, /device:TPU:0, one launch (start us, length us, event | category | flops | bytes accessed | tf_op | source)
XLA Modules:
  0.0 112.7 jit_solution(12949396784819274707)
XLA Ops:
  0.6 0.0 copy-start
  0.7 0.1 stack.39
  0.8 0.1 and.41
  0.9 0.1 and.42
  1.0 0.7 broadcast_compare_fusion
  1.6 0.1 broadcast_in_dim.25
  1.7 0.1 reshape.85
  1.9 0.1 and.36
  2.0 0.6 broadcast_in_dim.29.bias_ref
  2.7 3.3 %fusion.11 = bf16[3,10,36,256]{3,2,1,0:T(8,128)(2,1)S(1)} fusion(bf16[3,36,10,1536]{3,1,2,0:T(8,128)(2,1)} %param.11, bf16[256,1536]{1,0:T(8,128)(2,1)S(1)} %copy-done), kind=kOutput, calls=%fused_computation.8 | convolution fusion | flops 849623040 | bytes 4657152 | tf_op jit(solution)/shard_map/dot_general | solution.py:367
  6.0 0.0 copy-start.4
  6.0 0.2 reshape.99
  6.2 0.3 copy.30
  6.5 0.1 copy.31
  6.6 0.9 broadcast_select_fusion
  7.5 0.1 reshape.96
  7.6 0.1 copy.21
  7.8 0.7 pad.22.k_ref
  8.5 0.1 reshape.97
  8.6 0.1 copy.24
  8.8 0.7 pad.23.v_ref
  9.6 0.1 reshape.98
  9.7 0.1 copy.27
  9.8 0.7 pad.24.q_ref
  10.6 62.9 %query_side.1 = (bf16[4,272,128]{2,1,0:T(8,128)(2,1)}, bf16[4,272,128]{2,1,0:T(8,128)(2,1)}, bf16[4,272,128]{2,1,0:T(8,128)(2,1)}, bf16[4,2560,128]{2,1,0:T(8,12...) custom-call(bf16[4,272,128]{2,1,0:T(8,128)(2,1)} %pad.22.k_ref, bf16[4,272,128]{2,1,0:T(8,128)(2,1)} %pad.23.v_ref, ...), custom_call_target="tpu_custom_call" | custom-call | flops 14260633600 | bytes 5242880 | tf_op jit(solution)/shard_map/query_side/pallas_call | solution.py:390
  73.5 1.1 broadcast_select_fusion.2
  74.6 0.1 copy.32
  74.7 0.1 copy.58
  74.8 0.1 reshape.100
  74.9 0.8 constant_dynamic-update-slice_fusion.1
  75.7 0.1 copy.34
  75.8 0.1 copy.59
  76.0 0.1 reshape.101
  76.1 0.8 constant_dynamic-update-slice_fusion
  76.9 3.4 %fusion.8 = bf16[256,1536]{1,0:T(8,128)(2,1)S(1)} fusion(bf16[3,10,36,256]{3,2,1,0:T(8,128)(2,1)} %constant_dynamic-update-slice_fusion, bf16[3,36,10,1536]{3,1,2,0:T(8,128)(2,1)} %param.11), kind=kOutput, calls=%fused_computation.7 | convolution fusion | flops 849739776 | bytes 4657152 | tf_op jit(solution)/shard_map/dot_general | solution.py:427
  80.3 0.2 copy.40.live_ref
  80.6 24.2 %key_side.1 = (bf16[4,272,128]{2,1,0:T(8,128)(2,1)S(1)}, bf16[4,272,128]{2,1,0:T(8,128)(2,1)S(1)}, f32[16,1536]{1,0:T(8,128)S(1)}) custom-call(bf16[4,272,128]{2,1,0:T(8,128)(2,1)S(1)} %copy-done.1, bf16[4,272,128]{2,1,0:T(8,128)(2,1)S(1)} %copy-done.2, f32[4,272,1]{2,1,0:T(8,128)S(1)} %copy.40.live_ref, f32[4,8,2560]{2,1,0:T(8,128)S(1)} %copy-done.3, ...), custom_call_target="tpu_custom_call" | custom-call | flops 14260633600 | bytes 5242880 | tf_op jit(solution)/shard_map/key_side/pallas_call | solution.py:433
  104.8 0.1 copy.41
  105.0 0.1 reshape.90
  105.1 0.8 copy.46
  105.9 0.1 copy.43
  106.0 0.1 reshape.92
  106.1 0.8 copy.47
  106.9 4.0 %fusion.4 = bf16[3,36,10,1536]{3,1,2,0:T(8,128)(2,1)} fusion(bf16[3,10,36,256]{3,2,1,0:T(8,128)(2,1)} %constant_dynamic-update-slice_fusion, bf16[256,1536]{1,0:T(8,128)(2,1)S(1)} %copy-done), kind=kOutput, calls=%fused_computation.5 | convolution fusion | flops 851005440 | bytes 4657152 | tf_op jit(solution)/shard_map/dot_general | solution.py:422
  111.0 0.1 copy.38
  111.2 0.1 reshape.87
  111.2 0.8 copy.45
  112.0 0.6 copy.64
  (25 shorter events, 0.4 us)
Async XLA Ops:
  0.6 2.1 %copy-start = (bf16[256,1536]{1,0:T(8,128)(2,1)S(1)}, bf16[256,1536]{1,0:T(8,128)(2,1)}, u32[]{:S(2)}) copy-start(bf16[256,1536]{1,0:T(8,128)(2,1)} %param.10) | copy-start | bytes 2359300
  6.0 1.6 %copy-start.4 = (bf16[3,36,10,128]{3,1,2,0:T(8,128)(2,1)S(1)}, bf16[3,36,10,128]{3,1,2,0:T(8,128)(2,1)}, u32[]{:S(2)}) copy-start(bf16[3,36,10,128]{3,1,2,0:T(8,128)(2,1)} %param.7) | copy-start | bytes 829444
  6.0 2.6 %copy-start.5 = (bf16[3,36,10,128]{3,1,2,0:T(8,128)(2,1)S(1)}, bf16[3,36,10,128]{3,1,2,0:T(8,128)(2,1)}, u32[]{:S(2)}) copy-start(bf16[3,36,10,128]{3,1,2,0:T(8,128)(2,1)} %param.8) | copy-start | bytes 829444
  6.5 3.0 %copy-start.6 = (bf16[3,36,10,128]{3,1,2,0:T(8,128)(2,1)S(1)}, bf16[3,36,10,128]{3,1,2,0:T(8,128)(2,1)}, u32[]{:S(2)}) copy-start(bf16[3,36,10,128]{3,1,2,0:T(8,128)(2,1)} %param.6) | copy-start | bytes 829444
  75.9 4.6 %copy-start.1 = (bf16[4,272,128]{2,1,0:T(8,128)(2,1)S(1)}, bf16[4,272,128]{2,1,0:T(8,128)(2,1)}, u32[]{:S(2)}) copy-start(bf16[4,272,128]{2,1,0:T(8,128)(2,1)} %pad.22.k_ref) | copy-start | bytes 835588
  76.0 4.6 %copy-start.2 = (bf16[4,272,128]{2,1,0:T(8,128)(2,1)S(1)}, bf16[4,272,128]{2,1,0:T(8,128)(2,1)}, u32[]{:S(2)}) copy-start(bf16[4,272,128]{2,1,0:T(8,128)(2,1)} %pad.23.v_ref) | copy-start | bytes 835588
  76.0 4.6 %copy-start.3 = (f32[4,8,2560]{2,1,0:T(8,128)S(1)}, f32[4,8,2560]{2,1,0:T(8,128)}, u32[]{:S(2)}) copy-start(f32[4,8,2560]{2,1,0:T(8,128)} %get-tuple-element.17.stats_ref) | copy-start | bytes 983044
  106.0 5.0 %copy-start.7 = (bf16[4,272,128]{2,1,0:T(8,128)(2,1)S(1)}, bf16[4,272,128]{2,1,0:T(8,128)(2,1)}, u32[]{:S(2)}) copy-start(bf16[4,272,128]{2,1,0:T(8,128)(2,1)} %get-tuple-element.16) | copy-start | bytes 835588
